TPU v7x, 32 devices: a whole 2x2x4 slice. The times are simulated.
32 devices in a mesh: shot: 2 (over y), gx: 8 (over z, x), gy: 2 (over core).
Axes of the slice: x: 2, y: 2, z: 4, core: 2. Of those that a mesh axis runs over, the one named last changes fastest.
Arguments:
- fields_now: float32 [4, 64, 256, 128], P('shot', 'gx', 'gy'), parts along dimension 0, may hold values from -6 to 6
- fields_later: float32 [4, 64, 256, 128], P('shot', 'gx', 'gy'), parts along dimension 0, may hold values from -6 to 6
- velocity_term: float32 [64, 256, 128], P('gx', 'gy'), may hold values from 0.05 to 0.3
- damping: float32 [64, 256, 128], P('gx', 'gy'), may hold values from 0.005 to 0.3
- traces: float32 [6, 64, 256], P('shot', 'gx', 'gy'), parts along dimension 0, may hold values from -6 to 6
- receiver_live: int32 [64, 256], P('gx', 'gy'), may hold values from 0 to 1
Outputs:
- image_sum: float32 [34, 64, 256, 128], P('shot', 'gx', 'gy'), parts along dimension 0
There are 2 independent parts, one for each index of `shot`. A program takes and returns all parts, laid end to end along the dimension named above; an argument that names none is the same for every part. Nothing has to cross between parts.
All inputs are finite; a program needn't handle non-finite values.
Results may differ from a plain program's by a relative error of at most 0.00002.
Values sent between devices are 32-bit elements; how exact they have to be, the bound alone decides.
No kernel may reach another device: no remote copies, remote signals or barrier semaphores. Data moves between devices by JAX's collectives and lax.ppermute only.
A program may use at most 128 MiB of HBM per device.

v0:
```python
import jax
import jax.numpy as jnp
from jax import lax
from jax.sharding import PartitionSpec as P

STEPS = 4
LAG_HALF = 8


def padded(cells, sides, width):
    for axis, dim in sides:
        count = lax.axis_size(axis)
        ends = count - 1
        head = lax.slice_in_dim(cells, 0, width, axis=dim)
        tail = lax.slice_in_dim(cells, cells.shape[dim] - width, cells.shape[dim], axis=dim)
        cells = jnp.concatenate(
            [
                lax.ppermute(tail, axis, [(i, (i + 1) % count) for i in range(ends)]),
                cells,
                lax.ppermute(head, axis, [((i + 1) % count, i) for i in range(ends)]),
            ],
            axis=dim,
        )
    return cells


def lag_products(image_lags, slab, start, cells_x):
    updated = []
    for index, offset in enumerate(range(-LAG_HALF, LAG_HALF + 1)):
        left = slab[0, start - offset : start - offset + cells_x]
        right = slab[1, start + offset : start + offset + cells_x]
        updated.append(image_lags[index] + left * right)
    return updated


def source_mask(shape):
    channel_pick = (lax.broadcasted_iota(jnp.int32, shape, 0) == 1).astype(jnp.float32)
    surface = (lax.broadcasted_iota(jnp.int32, shape, 3) == 0).astype(jnp.float32)
    return channel_pick * surface


def shards(fields_now, fields_later, velocity_term, damping, traces, receiver_live):
    cells_x = fields_now.shape[1]
    live_mask = receiver_live.astype(jnp.float32)
    image_lags = [
        jnp.zeros(fields_now.shape[1:], jnp.float32) for offset in range(2 * LAG_HALF + 1)
    ]
    current = fields_now
    following = fields_later
    inject = source_mask(fields_now.shape)
    for time_step in range(STEPS):
        extended = padded(current, (("gx", 1),), LAG_HALF)
        image_lags = lag_products(image_lags, extended, LAG_HALF, cells_x)
        if time_step < STEPS - 1:
            crossed = padded(current, (("gy", 2),), 1)
            sum_x = (
                extended[:, LAG_HALF + 1 : LAG_HALF + 1 + cells_x]
                + extended[:, LAG_HALF - 1 : LAG_HALF - 1 + cells_x]
            )
            sum_y = crossed[:, :, 2:] + crossed[:, :, :-2]
            depth_pad = jnp.pad(current, ((0, 0), (0, 0), (0, 0), (1, 1)))
            sum_z = depth_pad[:, :, :, 2:] + depth_pad[:, :, :, :-2]
            source_plane = (live_mask * traces[time_step])[None, :, :, None]
            operated = sum_x + sum_y + sum_z - 6.0 * current + inject * source_plane
            earlier = (2.0 * current - (1.0 - damping) * following + velocity_term * operated) / (
                1.0 + damping
            )
            following = current
            current = earlier
    return jnp.stack(image_lags)


def solution(mesh):
    placed = (
        P("shot", "gx", "gy", None),
        P("shot", "gx", "gy", None),
        P("gx", "gy", None),
        P("gx", "gy", None),
        P("shot", "gx", "gy"),
        P("gx", "gy"),
    )
    return jax.shard_map(
        shards, mesh=mesh, in_specs=placed, out_specs=P("shot", "gx", "gy", None), check_vma=False
    )
```

profile of v0, /device:TPU:25, one launch (start us, length us, event | category | flops | bytes accessed | tf_op | source)
XLA Modules:
  0.0 215.6 jit_solution(15087082036846557840)
XLA Ops:
  0.0 3.2 %collective-permute-start.1 = (f32[2,8,128,128]{3,2,1,0:T(8,128)}, f32[2,8,128,128]{3,2,1,0:T(8,128)S(1)}, u32[]{:S(2)}, u32[]{:S(2)}) collective-permute-start(f32[2,8,128,128]{3,2,1,0:T(8,128)} %param.6), channel_id=1, source_target_pairs={{0,2},{2,4},{4,6},{6,8},{8,10},{10,12},{12,14},{1,3},{3,5},{5,7},{... | collective-permute-start | bytes 3145736 | tf_op jit(solution)/shard_map/ppermute | solution.py:18
  3.2 3.1 %collective-permute-start = (f32[2,8,128,128]{3,2,1,0:T(8,128)}, f32[2,8,128,128]{3,2,1,0:T(8,128)S(1)}, u32[]{:S(2)}, u32[]{:S(2)}) collective-permute-start(f32[2,8,128,128]{3,2,1,0:T(8,128)} %param.6), channel_id=1, source_target_pairs={{2,0},{4,2},{6,4},{8,6},{10,8},{12,10},{14,12},{3,1},{5,3},{7,5},{... | collective-permute-start | bytes 3145736 | tf_op jit(solution)/shard_map/ppermute | solution.py:20
  6.3 0.9 fusion.223
  7.2 3.1 %collective-permute-start.2 = (f32[2,8,1,128]{3,2,1,0:T(1,128)S(1)}, f32[2,8,1,128]{3,2,1,0:T(1,128)S(1)}, u32[]{:S(2)}, u32[]{:S(2)}) collective-permute-start(f32[2,8,1,128]{3,2,1,0:T(1,128)S(1)} %get-tuple-element.11), channel_id=1, source_target_pairs={{1,0},{3,2},{5,4},{7,6},{9,8},{11,10},{13,12},{15,14},{17,16},{19,... | collective-permute-start | bytes 24584 | tf_op jit(solution)/shard_map/ppermute | solution.py:20
  10.4 1.3 collective-permute-start.3
  11.7 0.7 bitcast_multiply_fusion
  12.4 1.1 broadcast_subtract_fusion
  13.6 13.6 %collective-permute-done.1 = f32[2,8,128,128]{3,2,1,0:T(8,128)S(1)} collective-permute-done((f32[2,8,128,128]{3,2,1,0:T(8,128)}, f32[2,8,128,128]{3,2,1,0:T(8,128)S(1)}, u32[]{:S(2)}, u32[]{:S(2)}) %collective-permute-start.1) | collective-permute-done | bytes 1048608 | tf_op jit(solution)/shard_map/ppermute | solution.py:18
  27.6 23.1 %collective-permute-done = f32[2,8,128,128]{3,2,1,0:T(8,128)S(1)} collective-permute-done((f32[2,8,128,128]{3,2,1,0:T(8,128)}, f32[2,8,128,128]{3,2,1,0:T(8,128)S(1)}, u32[]{:S(2)}, u32[]{:S(2)}) %collective-permute-start) | collective-permute-done | bytes 1048608 | tf_op jit(solution)/shard_map/ppermute | solution.py:20
  50.8 1.1 fusion.3
  51.9 1.9 collective-permute-start.5
  53.8 4.3 %collective-permute-start.4 = (f32[2,8,128,128]{3,2,1,0:T(8,128)S(1)}, f32[2,8,128,128]{3,2,1,0:T(8,128)S(1)}, u32[]{:S(2)}, u32[]{:S(2)}) collective-permute-start(f32[2,8,128,128]{3,2,1,0:T(8,128)S(1)} %fusion.3), channel_id=1, source_target_pairs={{2,0},{4,2},{6,4},{8,6},{10,8},{12,10},{14,12},{3,1},{5,3},{7,5},{... | collective-permute-start | bytes 3145736 | tf_op jit(solution)/shard_map/ppermute | solution.py:20
  58.1 3.0 %collective-permute-start.6 = (f32[2,8,1,128]{3,2,1,0:T(1,128)S(1)}, f32[2,8,1,128]{3,2,1,0:T(1,128)S(1)}, u32[]{:S(2)}, u32[]{:S(2)}) collective-permute-start(f32[2,8,1,128]{3,2,1,0:T(1,128)S(1)} %get-tuple-element.7), channel_id=1, source_target_pairs={{1,0},{3,2},{5,4},{7,6},{9,8},{11,10},{13,12},{15,14},{17,16},{19,... | collective-permute-start | bytes 24584 | tf_op jit(solution)/shard_map/ppermute | solution.py:20
  61.1 1.3 collective-permute-start.7
  62.4 1.8 collective-permute-done.7
  64.1 14.8 %collective-permute-done.5 = f32[2,8,128,128]{3,2,1,0:T(8,128)S(1)} collective-permute-done((f32[2,8,128,128]{3,2,1,0:T(8,128)S(1)}, f32[2,8,128,128]{3,2,1,0:T(8,128)S(1)}, u32[]{:S(2)}, u32[]{:S(2)}) %collective-permute-start.5) | collective-permute-done | bytes 1048608 | tf_op jit(solution)/shard_map/ppermute | solution.py:18
  79.0 23.3 %collective-permute-done.4 = f32[2,8,128,128]{3,2,1,0:T(8,128)S(1)} collective-permute-done((f32[2,8,128,128]{3,2,1,0:T(8,128)S(1)}, f32[2,8,128,128]{3,2,1,0:T(8,128)S(1)}, u32[]{:S(2)}, u32[]{:S(2)}) %collective-permute-start.4) | collective-permute-done | bytes 1048608 | tf_op jit(solution)/shard_map/ppermute | solution.py:20
  102.2 1.4 fusion.7
  103.6 1.9 collective-permute-start.9
  105.5 4.3 %collective-permute-start.8 = (f32[2,8,128,128]{3,2,1,0:T(8,128)S(1)}, f32[2,8,128,128]{3,2,1,0:T(8,128)S(1)}, u32[]{:S(2)}, u32[]{:S(2)}) collective-permute-start(f32[2,8,128,128]{3,2,1,0:T(8,128)S(1)} %fusion.7), channel_id=1, source_target_pairs={{2,0},{4,2},{6,4},{8,6},{10,8},{12,10},{14,12},{3,1},{5,3},{7,5},{... | collective-permute-start | bytes 3145736 | tf_op jit(solution)/shard_map/ppermute | solution.py:20
  109.8 3.0 %collective-permute-start.10 = (f32[2,8,1,128]{3,2,1,0:T(1,128)S(1)}, f32[2,8,1,128]{3,2,1,0:T(1,128)S(1)}, u32[]{:S(2)}, u32[]{:S(2)}) collective-permute-start(f32[2,8,1,128]{3,2,1,0:T(1,128)S(1)} %get-tuple-element.5), channel_id=1, source_target_pairs={{1,0},{3,2},{5,4},{7,6},{9,8},{11,10},{13,12},{15,14},{17,16},{19,... | collective-permute-start | bytes 24584 | tf_op jit(solution)/shard_map/ppermute | solution.py:20
  112.8 1.3 collective-permute-start.11
  114.1 1.8 collective-permute-done.11
  115.9 14.8 %collective-permute-done.9 = f32[2,8,128,128]{3,2,1,0:T(8,128)S(1)} collective-permute-done((f32[2,8,128,128]{3,2,1,0:T(8,128)S(1)}, f32[2,8,128,128]{3,2,1,0:T(8,128)S(1)}, u32[]{:S(2)}, u32[]{:S(2)}) %collective-permute-start.9) | collective-permute-done | bytes 1048608 | tf_op jit(solution)/shard_map/ppermute | solution.py:18
  130.7 23.3 %collective-permute-done.8 = f32[2,8,128,128]{3,2,1,0:T(8,128)S(1)} collective-permute-done((f32[2,8,128,128]{3,2,1,0:T(8,128)S(1)}, f32[2,8,128,128]{3,2,1,0:T(8,128)S(1)}, u32[]{:S(2)}, u32[]{:S(2)}) %collective-permute-start.8) | collective-permute-done | bytes 1048608 | tf_op jit(solution)/shard_map/ppermute | solution.py:20
  154.0 1.3 fusion.11
  155.3 1.9 collective-permute-start.13
  157.2 4.3 %collective-permute-start.12 = (f32[2,8,128,128]{3,2,1,0:T(8,128)S(1)}, f32[2,8,128,128]{3,2,1,0:T(8,128)S(1)}, u32[]{:S(2)}, u32[]{:S(2)}) collective-permute-start(f32[2,8,128,128]{3,2,1,0:T(8,128)S(1)} %fusion.11), channel_id=1, source_target_pairs={{2,0},{4,2},{6,4},{8,6},{10,8},{12,10},{14,12},{3,1},{5,3},{7,5},{... | collective-permute-start | bytes 3145736 | tf_op jit(solution)/shard_map/ppermute | solution.py:20
  161.5 20.9 %collective-permute-done.13 = f32[2,8,128,128]{3,2,1,0:T(8,128)S(1)} collective-permute-done((f32[2,8,128,128]{3,2,1,0:T(8,128)S(1)}, f32[2,8,128,128]{3,2,1,0:T(8,128)S(1)}, u32[]{:S(2)}, u32[]{:S(2)}) %collective-permute-start.13) | collective-permute-done | bytes 1048608 | tf_op jit(solution)/shard_map/ppermute | solution.py:18
  182.4 23.3 %collective-permute-done.12 = f32[2,8,128,128]{3,2,1,0:T(8,128)S(1)} collective-permute-done((f32[2,8,128,128]{3,2,1,0:T(8,128)S(1)}, f32[2,8,128,128]{3,2,1,0:T(8,128)S(1)}, u32[]{:S(2)}, u32[]{:S(2)}) %collective-permute-start.12) | collective-permute-done | bytes 1048608 | tf_op jit(solution)/shard_map/ppermute | solution.py:20
  205.7 0.3 fusion.218
  206.0 0.3 fusion.40
  206.3 0.3 fusion.44
  206.7 0.3 fusion.48
  207.0 0.3 fusion.52
  207.3 0.3 fusion.56
  207.6 0.3 fusion.60
  208.0 0.3 fusion.64
  208.3 0.3 fusion.214
  208.6 0.3 fusion.68
  208.9 0.3 fusion.72
  209.3 0.3 fusion.76
  209.6 0.3 fusion.80
  209.9 0.3 fusion.84
  210.2 0.3 fusion.36
  210.6 0.3 fusion.208
  210.9 3.6 %copy-done.3 = f32[17,8,128,128]{3,2,1,0:T(8,128)} copy-done((f32[17,8,128,128]{3,2,1,0:T(8,128)}, f32[17,8,128,128]{3,2,1,0:T(8,128)S(1)}, u32[]{:S(2)}) %copy-start.3) | copy-done | bytes 8912920
  214.5 1.1 fusion.203
  (18 shorter events, 0.5 us)
Async XLA Ops:
  0.0 27.3 %copy-start = (f32[2,8,128,128]{3,2,1,0:T(8,128)S(1)}, f32[2,8,128,128]{3,2,1,0:T(8,128)}, u32[]{:S(2)}) copy-start(f32[2,8,128,128]{3,2,1,0:T(8,128)} %param.6) | copy-start | bytes 3145732
  0.0 27.2 %collective-permute-start.1 = (f32[2,8,128,128]{3,2,1,0:T(8,128)}, f32[2,8,128,128]{3,2,1,0:T(8,128)S(1)}, u32[]{:S(2)}, u32[]{:S(2)}) collective-permute-start(f32[2,8,128,128]{3,2,1,0:T(8,128)} %param.6), channel_id=1, source_target_pairs={{0,2},{2,4},{4,6},{6,8},{8,10},{10,12},{12,14},{1,3},{3,5},{5,7},{... | collective-permute-start | bytes 3145736 | tf_op jit(solution)/shard_map/ppermute | solution.py:18
  3.2 47.4 %collective-permute-start = (f32[2,8,128,128]{3,2,1,0:T(8,128)}, f32[2,8,128,128]{3,2,1,0:T(8,128)S(1)}, u32[]{:S(2)}, u32[]{:S(2)}) collective-permute-start(f32[2,8,128,128]{3,2,1,0:T(8,128)} %param.6), channel_id=1, source_target_pairs={{2,0},{4,2},{6,4},{8,6},{10,8},{12,10},{14,12},{3,1},{5,3},{7,5},{... | collective-permute-start | bytes 3145736 | tf_op jit(solution)/shard_map/ppermute | solution.py:20
  7.2 43.6 %collective-permute-start.2 = (f32[2,8,1,128]{3,2,1,0:T(1,128)S(1)}, f32[2,8,1,128]{3,2,1,0:T(1,128)S(1)}, u32[]{:S(2)}, u32[]{:S(2)}) collective-permute-start(f32[2,8,1,128]{3,2,1,0:T(1,128)S(1)} %get-tuple-element.11), channel_id=1, source_target_pairs={{1,0},{3,2},{5,4},{7,6},{9,8},{11,10},{13,12},{15,14},{17,16},{19,... | collective-permute-start | bytes 24584 | tf_op jit(solution)/shard_map/ppermute | solution.py:20
  10.4 40.4 %collective-permute-start.3 = (f32[2,8,1,128]{3,2,1,0:T(1,128)S(1)}, f32[2,8,1,128]{3,2,1,0:T(1,128)S(1)}, u32[]{:S(2)}, u32[]{:S(2)}) collective-permute-start(f32[2,8,1,128]{3,2,1,0:T(1,128)S(1)} %get-tuple-element.12), channel_id=1, source_target_pairs={{0,1},{2,3},{4,5},{6,7},{8,9},{10,11},{12,13},{14,15},{16,17},{18,... | collective-permute-start | bytes 24584 | tf_op jit(solution)/shard_map/ppermute | solution.py:18
  27.3 23.5 %copy-start.1 = (f32[8,128,128]{2,1,0:T(8,128)S(1)}, f32[8,128,128]{2,1,0:T(8,128)}, u32[]{:S(2)}) copy-start(f32[8,128,128]{2,1,0:T(8,128)} %param.8) | copy-start | bytes 1572868
  27.3 23.5 %copy-start.2 = (f32[2,8,128,128]{3,2,1,0:T(8,128)S(1)}, f32[2,8,128,128]{3,2,1,0:T(8,128)}, u32[]{:S(2)}) copy-start(f32[2,8,128,128]{3,2,1,0:T(8,128)} %param.7) | copy-start | bytes 3145732
  51.9 27.1 %collective-permute-start.5 = (f32[2,8,128,128]{3,2,1,0:T(8,128)S(1)}, f32[2,8,128,128]{3,2,1,0:T(8,128)S(1)}, u32[]{:S(2)}, u32[]{:S(2)}) collective-permute-start(f32[2,8,128,128]{3,2,1,0:T(8,128)S(1)} %fusion.3), channel_id=1, source_target_pairs={{0,2},{2,4},{4,6},{6,8},{8,10},{10,12},{12,14},{1,3},{3,5},{5,7},{... | collective-permute-start | bytes 3145736 | tf_op jit(solution)/shard_map/ppermute | solution.py:18
  53.8 48.4 %collective-permute-start.4 = (f32[2,8,128,128]{3,2,1,0:T(8,128)S(1)}, f32[2,8,128,128]{3,2,1,0:T(8,128)S(1)}, u32[]{:S(2)}, u32[]{:S(2)}) collective-permute-start(f32[2,8,128,128]{3,2,1,0:T(8,128)S(1)} %fusion.3), channel_id=1, source_target_pairs={{2,0},{4,2},{6,4},{8,6},{10,8},{12,10},{14,12},{3,1},{5,3},{7,5},{... | collective-permute-start | bytes 3145736 | tf_op jit(solution)/shard_map/ppermute | solution.py:20
  58.1 4.3 %collective-permute-start.6 = (f32[2,8,1,128]{3,2,1,0:T(1,128)S(1)}, f32[2,8,1,128]{3,2,1,0:T(1,128)S(1)}, u32[]{:S(2)}, u32[]{:S(2)}) collective-permute-start(f32[2,8,1,128]{3,2,1,0:T(1,128)S(1)} %get-tuple-element.7), channel_id=1, source_target_pairs={{1,0},{3,2},{5,4},{7,6},{9,8},{11,10},{13,12},{15,14},{17,16},{19,... | collective-permute-start | bytes 24584 | tf_op jit(solution)/shard_map/ppermute | solution.py:20
  61.1 3.1 %collective-permute-start.7 = (f32[2,8,1,128]{3,2,1,0:T(1,128)S(1)}, f32[2,8,1,128]{3,2,1,0:T(1,128)S(1)}, u32[]{:S(2)}, u32[]{:S(2)}) collective-permute-start(f32[2,8,1,128]{3,2,1,0:T(1,128)S(1)} %get-tuple-element.8), channel_id=1, source_target_pairs={{0,1},{2,3},{4,5},{6,7},{8,9},{10,11},{12,13},{14,15},{16,17},{18,... | collective-permute-start | bytes 24584 | tf_op jit(solution)/shard_map/ppermute | solution.py:18
  103.6 27.1 %collective-permute-start.9 = (f32[2,8,128,128]{3,2,1,0:T(8,128)S(1)}, f32[2,8,128,128]{3,2,1,0:T(8,128)S(1)}, u32[]{:S(2)}, u32[]{:S(2)}) collective-permute-start(f32[2,8,128,128]{3,2,1,0:T(8,128)S(1)} %fusion.7), channel_id=1, source_target_pairs={{0,2},{2,4},{4,6},{6,8},{8,10},{10,12},{12,14},{1,3},{3,5},{5,7},{... | collective-permute-start | bytes 3145736 | tf_op jit(solution)/shard_map/ppermute | solution.py:18
  105.5 48.4 %collective-permute-start.8 = (f32[2,8,128,128]{3,2,1,0:T(8,128)S(1)}, f32[2,8,128,128]{3,2,1,0:T(8,128)S(1)}, u32[]{:S(2)}, u32[]{:S(2)}) collective-permute-start(f32[2,8,128,128]{3,2,1,0:T(8,128)S(1)} %fusion.7), channel_id=1, source_target_pairs={{2,0},{4,2},{6,4},{8,6},{10,8},{12,10},{14,12},{3,1},{5,3},{7,5},{... | collective-permute-start | bytes 3145736 | tf_op jit(solution)/shard_map/ppermute | solution.py:20
  109.8 4.3 %collective-permute-start.10 = (f32[2,8,1,128]{3,2,1,0:T(1,128)S(1)}, f32[2,8,1,128]{3,2,1,0:T(1,128)S(1)}, u32[]{:S(2)}, u32[]{:S(2)}) collective-permute-start(f32[2,8,1,128]{3,2,1,0:T(1,128)S(1)} %get-tuple-element.5), channel_id=1, source_target_pairs={{1,0},{3,2},{5,4},{7,6},{9,8},{11,10},{13,12},{15,14},{17,16},{19,... | collective-permute-start | bytes 24584 | tf_op jit(solution)/shard_map/ppermute | solution.py:20
  112.8 3.1 %collective-permute-start.11 = (f32[2,8,1,128]{3,2,1,0:T(1,128)S(1)}, f32[2,8,1,128]{3,2,1,0:T(1,128)S(1)}, u32[]{:S(2)}, u32[]{:S(2)}) collective-permute-start(f32[2,8,1,128]{3,2,1,0:T(1,128)S(1)} %get-tuple-element.6), channel_id=1, source_target_pairs={{0,1},{2,3},{4,5},{6,7},{8,9},{10,11},{12,13},{14,15},{16,17},{18,... | collective-permute-start | bytes 24584 | tf_op jit(solution)/shard_map/ppermute | solution.py:18
  155.3 27.1 %collective-permute-start.13 = (f32[2,8,128,128]{3,2,1,0:T(8,128)S(1)}, f32[2,8,128,128]{3,2,1,0:T(8,128)S(1)}, u32[]{:S(2)}, u32[]{:S(2)}) collective-permute-start(f32[2,8,128,128]{3,2,1,0:T(8,128)S(1)} %fusion.11), channel_id=1, source_target_pairs={{0,2},{2,4},{4,6},{6,8},{8,10},{10,12},{12,14},{1,3},{3,5},{5,7},{... | collective-permute-start | bytes 3145736 | tf_op jit(solution)/shard_map/ppermute | solution.py:18
  157.2 48.4 %collective-permute-start.12 = (f32[2,8,128,128]{3,2,1,0:T(8,128)S(1)}, f32[2,8,128,128]{3,2,1,0:T(8,128)S(1)}, u32[]{:S(2)}, u32[]{:S(2)}) collective-permute-start(f32[2,8,128,128]{3,2,1,0:T(8,128)S(1)} %fusion.11), channel_id=1, source_target_pairs={{2,0},{4,2},{6,4},{8,6},{10,8},{12,10},{14,12},{3,1},{5,3},{7,5},{... | collective-permute-start | bytes 3145736 | tf_op jit(solution)/shard_map/ppermute | solution.py:20
  210.9 3.6 %copy-start.3 = (f32[17,8,128,128]{3,2,1,0:T(8,128)}, f32[17,8,128,128]{3,2,1,0:T(8,128)S(1)}, u32[]{:S(2)}) copy-start(f32[17,8,128,128]{3,2,1,0:T(8,128)S(1)} %fusion.208) | copy-start | bytes 26738692
where the time goes:
time: 216 us
  waiting for transfers between devices  161 us (75%)
  starting transfers between devices  37.8 us (17%)
  other arithmetic  12 us (6%)
  local copies, waits for them, and re-layouts  4.92 us (2%)
    ppermute x7, waiting for transfers between devices, padded(): lax.ppermute(head, axis, [((i + 1) % count, i) for i in range(ends)])  92.9 us
    ppermute x7, waiting for transfers between devices, padded(): lax.ppermute(tail, axis, [(i, (i + 1) % count) for i in range(ends)])  67.7 us
    ppermute x7, starting transfers between devices, padded(): lax.ppermute(head, axis, [((i + 1) % count, i) for i in range(ends)])  24.9 us
    ppermute x7, starting transfers between devices, padded(): lax.ppermute(tail, axis, [(i, (i + 1) % count) for i in range(ends)])  12.9 us
    unnamed x16, other arithmetic  5.21 us
  transfers between devices with their start and end apart: 14, of which 10 were waited for; matrix products, arithmetic and copies ran while one was open for 1% of the time, Pallas kernels for 0%

commit v1 on v0

--- a/solution.py
+++ b/solution.py
@@ -1,10 +1,14 @@
+import functools
 import jax
 import jax.numpy as jnp
 from jax import lax
+from jax.experimental import pallas as pl
+from jax.experimental.pallas import tpu as pltpu
 from jax.sharding import PartitionSpec as P
 
 STEPS = 4
 LAG_HALF = 8
+CHUNKS = (48, 48, 32)
 
 
 def padded(cells, sides, width):
@@ -39,7 +43,7 @@
     return channel_pick * surface
 
 
-def shards(fields_now, fields_later, velocity_term, damping, traces, receiver_live):
+def plain(fields_now, fields_later, velocity_term, damping, traces, receiver_live):
     cells_x = fields_now.shape[1]
     live_mask = receiver_live.astype(jnp.float32)
     image_lags = [
@@ -70,6 +74,499 @@
     return jnp.stack(image_lags)
 
 
+X = 8
+Y = 128
+Z = 128
+G = 8
+F32 = jnp.float32
+HBM = pl.BlockSpec(memory_space=pltpu.HBM)
+VMEM = pl.BlockSpec(memory_space=pltpu.VMEM)
+
+
+def by8(value):
+    return pl.multiple_of(value, G)
+
+
+def place():
+    even = lax.axis_index("gx") % 2 == 0
+    return even, lax.axis_index("gy"), lax.axis_index("shot")
+
+
+def run_copies(pieces, sem):
+    copies = [pltpu.make_async_copy(a, b, sem.at[j]) for j, (a, b) in enumerate(pieces)]
+    for c in copies:
+        c.start()
+    return copies
+
+
+def wait_all(copies):
+    for c in copies:
+        c.wait()
+
+
+def shifted(ref, f, row, lo, size, first, last):
+    centre = ref[f, row, lo : lo + size]
+    total = ref[f, row - 1, lo : lo + size] + ref[f, row + 1, lo : lo + size]
+    total += ref[f, row, lo - 1 : lo - 1 + size] + ref[f, row, lo + 1 : lo + 1 + size]
+    total += jnp.where(first, 0.0, pltpu.roll(centre, 1, 1))
+    total += jnp.where(last, 0.0, pltpu.roll(centre, Z - 1, 1))
+    return centre, total
+
+
+def coefficients(vel, damp):
+    inv = 1.0 / (1.0 + damp)
+    gain = vel * inv
+    return (1.0 - damp) * inv, gain, 2.0 * inv - 6.0 * gain
+
+
+def prep_kernel(u0, v, d, traces, live, edge, rest, mine, on0, brink, t, sem):
+    even, gy, shot = place()
+    row = jnp.where(even, X - 1, 0)
+    y = by8(jnp.where(gy == 0, Y - G, 0))
+    for n in range(2):
+        t[n] = live[...].astype(F32) * traces[n + 1]
+    own = pl.ds(0, Y)
+    pieces = [
+        (u0.at[:, 0], edge.at[:, 0, own]),
+        (u0.at[:, X - 1], edge.at[:, 1, own]),
+        (t.at[0], edge.at[0, 0, pl.ds(Y, G)]),
+        (t.at[1], edge.at[0, 1, pl.ds(Y, G)]),
+        (u0.at[:, :, pl.ds(y, G)], brink),
+        (u0.at[:, row], on0.at[pl.ds(0, 2), own]),
+        (v.at[row], on0.at[2, own]),
+        (d.at[row], on0.at[3, own]),
+        (t.at[0], on0.at[0, pl.ds(Y, G)]),
+        (t.at[1], on0.at[1, pl.ds(Y, G)]),
+        (u0.at[:, pl.ds(1, 6)], rest),
+    ]
+    copies = run_copies(pieces, sem)
+
+    @pl.when(shot == 0)
+    def _():
+        pltpu.make_async_copy(v, mine, sem.at[len(pieces)]).start()
+
+    @pl.when(shot != 0)
+    def _():
+        pltpu.make_async_copy(d, mine, sem.at[len(pieces)]).start()
+
+    wait_all(copies)
+    pltpu.make_async_copy(v, mine, sem.at[len(pieces)]).wait()
+
+
+def surface_columns(rows):
+    wide = jnp.concatenate([rows, jnp.zeros((Z - rows.shape[0], Y), F32)], 0)
+    return wide.T
+
+
+def first_kernel(chunks, *args):
+    u0, later, v, d, near_e, far_e, beside, traces, live = args[:9]
+    u1, on1, back = args[9:12]
+    parts = args[12 : 12 + len(chunks)]
+    c, f0, vel, damp, out, t, sem = args[12 + len(chunks) :]
+    even, gy, shot = place()
+    own = pl.ds(0, Y)
+    near_pick, near_row = jnp.where(even, 0, 1), jnp.where(even, 9, 0)
+    far_pick, far_row = jnp.where(even, 1, 0), jnp.where(even, 0, 9)
+    mid = pl.ds(G, Y)
+    at = by8(jnp.where(gy == 0, Y + G, 0))
+    copies = run_copies(
+        [
+            (u0, c.at[:, pl.ds(1, X), mid]),
+            (near_e.at[:, near_pick, own], c.at[:, near_row, mid]),
+            (far_e.at[:, far_pick, own], c.at[:, far_row, mid]),
+            (beside, c.at[:, pl.ds(1, X), pl.ds(at, G)]),
+            (later, f0),
+            (v, vel),
+            (d, damp),
+        ],
+        sem,
+    )
+    rim = by8(jnp.where(gy == 0, 0, Y + G))
+    for f in range(2):
+        for x in range(X):
+            c[f, x + 1, pl.ds(rim, G)] = jnp.zeros((G, Z), F32)
+    mask = live[...].astype(F32)
+    for n in range(2):
+        t[n] = mask * traces[n + 1]
+    column = surface_columns(mask * traces[0])
+    wait_all(copies)
+    row = jnp.where(even, 0, X - 1)
+    early = run_copies(
+        [
+            (c.at[:, row + 1, mid], back.at[pl.ds(0, 2), own]),
+            (vel.at[row], back.at[2, own]),
+            (damp.at[row], back.at[3, own]),
+            (t.at[0], back.at[0, pl.ds(Y, G)]),
+            (t.at[1], back.at[1, pl.ds(Y, G)]),
+        ],
+        sem,
+    )
+    lane = lax.broadcasted_iota(jnp.int32, (Y, Z), 1)
+    first, last = lane == 0, lane == Z - 1
+    for x in range(X):
+        pull, gain, keep = coefficients(vel[x], damp[x])
+        for f in range(2):
+            centre, total = shifted(c, f, x + 1, G, Y, first, last)
+            if f == 1:
+                turned = pltpu.roll(column, Z - x, 1) if x else column
+                total += jnp.where(first, turned, 0.0)
+            out[f, x] = keep * centre - pull * f0[f, x] + gain * total
+    wait_all(early)
+    away = pl.ds(jnp.where(even, 6, 0), 2)
+    toward = jnp.where(even, 0, 6)
+    pieces = [(out, u1), (out.at[:, away], on1)]
+    for f in range(2):
+        pieces.append((out.at[f, pl.ds(toward, 2)], back.at[pl.ds(4 + 2 * f, 2), own]))
+    begin = 0
+    for width, part in zip(chunks, parts):
+        y = by8(jnp.where(gy == 1, begin, Y - begin - width))
+        pieces.append((out.at[:, :, pl.ds(y, width)], part))
+        begin += width
+    wait_all(run_copies(pieces, sem))
+
+
+NAMES0 = ("ne", "nr", "na", "nb", "fe", "fr", "fa", "fb", "u0", "v", "d", "on", "back")
+NAMES1 = ("u1", "on1")
+
+
+def level0_pieces(refs, u0, co, src, dst, size, even, shot):
+    near, far = jnp.where(even, 17, 1), jnp.where(even, 1, 17)
+    s, d = pl.ds(src, size), pl.ds(dst, size)
+    out = []
+    for base, edge, rest, mine, other in (
+        (near, refs["ne"], refs["nr"], refs["na"], refs["nb"]),
+        (far, refs["fe"], refs["fr"], refs["fa"], refs["fb"]),
+    ):
+        out.append((edge.at[:, 0, s], u0(base, None, d)))
+        out.append((edge.at[:, 1, s], u0(base + 7, None, d)))
+        out.append((rest.at[:, :, s], u0(base + 1, 6, d)))
+        out.append((mine.at[:, s], co(base, X, d, shot)))
+        out.append((other.at[:, s], co(base, X, d, 1 - shot)))
+    out.append((refs["u0"].at[:, :, s], u0(9, X, d)))
+    out.append((refs["v"].at[:, s], co(9, X, d, 0)))
+    out.append((refs["d"].at[:, s], co(9, X, d, 1)))
+    for row, part in ((jnp.where(even, 0, 25), refs["on"]), (jnp.where(even, 25, 0), refs["back"])):
+        out.append((part.at[pl.ds(0, 2), s], u0(row, None, d)))
+        out.append((part.at[pl.ds(2, 2), s], co(row, None, d, None)))
+    return out
+
+
+def target(ref):
+    def pick(row, rows, d, lead=None):
+        lead = slice(None) if lead is None else lead
+        return ref.at[lead, row if rows is None else pl.ds(row, rows), d]
+
+    return pick
+
+
+def level1_own(refs, u1, src, dst, size, even):
+    s, d = pl.ds(src, size), pl.ds(dst, size)
+    on, back = jnp.where(even, 0, 26), jnp.where(even, 26, 0)
+    out = [
+        (refs["u1"].at[:, :, s], u1.at[:, pl.ds(10, X), d]),
+        (refs["on1"].at[:, :, s], u1.at[:, pl.ds(on, 2), d]),
+    ]
+    for f in range(2):
+        out.append((refs["back"].at[pl.ds(4 + 2 * f, 2), s], u1.at[f, pl.ds(back, 2), d]))
+    return out
+
+
+def level1_chunk(near_ref, far_ref, u1, src, dst, size, even):
+    near, far = jnp.where(even, 18, 2), jnp.where(even, 2, 18)
+    s, d = pl.ds(src, size), pl.ds(dst, size)
+    return [
+        (near_ref.at[:, :, s], u1.at[:, pl.ds(near, X), d]),
+        (far_ref.at[:, :, s], u1.at[:, pl.ds(far, X), d]),
+    ]
+
+
+def rim0_kernel(*args):
+    refs = dict(zip(NAMES0, args))
+    traces, live, rim, columns, rows, u0, co, sem = args[len(NAMES0) :]
+    even, gy, shot = place()
+    y = by8(jnp.where(gy == 0, Y - G, 0))
+    pieces = level0_pieces(refs, target(u0), target(co), y, 0, G, even, shot)
+    for part, at in (
+        (refs["ne"], jnp.where(even, 24, 8)),
+        (refs["fe"], jnp.where(even, 8, 24)),
+        (refs["on"], jnp.where(even, 0, 32)),
+        (refs["back"], jnp.where(even, 32, 0)),
+    ):
+        for n in range(2):
+            spot = part.at[0, n] if len(part.shape) == 4 else part.at[n]
+            pieces.append((spot.at[pl.ds(Y, G)], rows.at[n, pl.ds(by8(at), X)]))
+    copies = run_copies(pieces, sem)
+    mask = live[...].astype(F32)
+    for n in range(2):
+        rows[n, 16:24] = mask * traces[n + 1]
+    wait_all(copies)
+    for f in range(2):
+        rim[26 * f : 26 * f + 26] = u0[f]
+        rim[52 + 26 * f : 78 + 26 * f] = co[f]
+    for n in range(2):
+        columns[n] = surface_columns(rows[n])
+        rim[104 + n] = columns[n, pl.ds(y, G)]
+
+
+def rim1_kernel(chunk, *args):
+    refs = dict(zip(("u1", "on1", "back"), args))
+    near, far, out, sem = args[3:]
+    even, gy, shot = place()
+    y = by8(jnp.where(gy == 0, Y - G, 0))
+    yc = by8(jnp.where(gy == 0, chunk - G, 0))
+    pieces = level1_own(refs, out, y, 0, G, even) + level1_chunk(near, far, out, yc, 0, G, even)
+    wait_all(run_copies(pieces, sem))
+
+
+def slab_kernel(k, chunks, *args):
+    n_in = len(NAMES0) + len(NAMES1)
+    refs = dict(zip(NAMES0 + NAMES1, args[:n_in]))
+    rest = list(args[n_in:])
+    columns = rest.pop(0)
+    near_k, far_k = rest.pop(0), rest.pop(0)
+    first_slab, last_slab = k == 0, k == len(chunks) - 1
+    if first_slab:
+        rim0, rim1 = rest.pop(0), rest.pop(0)
+    else:
+        near_p, far_p, _ = rest.pop(0), rest.pop(0), rest.pop(0)
+    out_hbm, u0, u1, u2, u3, co, abc, inj, image, sem, out_sem = rest
+    even, gy, shot = place()
+    start, width = sum(chunks[:k]), chunks[k]
+    lead = G if first_slab else 2 * G
+    span = lead + width + (G if last_slab else 0)
+    size = span - 2 * G
+
+    def spot(at, length, total):
+        return by8(jnp.where(gy == 1, at, total - at - length))
+
+    ahead = 0 if first_slab else 2 * G
+    src = spot(start - ahead, ahead + width, Y)
+    here = spot(lead - ahead, ahead + width, span)
+    dst = by8(here + G)
+    pieces = level0_pieces(refs, target(u0), target(co), src, dst, ahead + width, even, shot)
+    pieces += level1_own(refs, u1, src, dst, ahead + width, even)
+    pieces.append((columns.at[:, pl.ds(src, ahead + width)], inj.at[:, pl.ds(here, ahead + width)]))
+    at = by8(spot(lead, width, span) + G)
+    pieces += level1_chunk(near_k, far_k, u1, 0, at, width, even)
+    if first_slab:
+        at = by8(spot(0, G, span) + G)
+        pieces.append((rim1, u1.at[:, :, pl.ds(at, G)]))
+        for f in range(2):
+            pieces.append((rim0.at[pl.ds(26 * f, 26)], u0.at[f, :, pl.ds(at, G)]))
+            pieces.append((rim0.at[pl.ds(52 + 26 * f, 26)], co.at[f, :, pl.ds(at, G)]))
+        pieces.append((rim0.at[pl.ds(104, 2)], inj.at[:, pl.ds(by8(spot(0, G, span)), G)]))
+    else:
+        before = chunks[k - 1]
+        at = by8(spot(0, 2 * G, span) + G)
+        pieces += level1_chunk(
+            near_p, far_p, u1, spot(before - 2 * G, 2 * G, before), at, 2 * G, even
+        )
+    copies = run_copies(pieces, sem)
+    if last_slab:
+        edge = spot(span - G, G, span)
+        for ref in (u0, u1, co):
+            for j in range(ref.shape[1]):
+                ref[:, j, pl.ds(by8(edge + G), G)] = jnp.zeros((2, G, Z), F32)
+        inj[:, pl.ds(edge, G)] = jnp.zeros((2, G, Z), F32)
+    wait_all(copies)
+
+    lane = lax.broadcasted_iota(jnp.int32, (span, Z), 1)
+    first, last = lane == 0, lane == Z - 1
+    y = slice(G, G + span)
+
+    def second(row, carry):
+        pull, gain, keep = coefficients(co[0, row, y], co[1, row, y])
+        abc[0, row, y] = pull
+        abc[1, row, y] = gain
+        abc[2, row, y] = keep
+        for f in range(2):
+            centre, total = shifted(u1, f, row + 1, G, span, first, last)
+            if f == 1:
+                total += jnp.where(first, pltpu.roll(inj[0], 121 - row, 1), 0.0)
+            u2[f, row, y] = keep * centre - pull * u0[f, row, y] + gain * total
+        return carry
+
+    lax.fori_loop(0, 26, second, 0, unroll=13)
+    first_, last_ = first[:size], last[:size]
+    yy = slice(2 * G, 2 * G + size)
+
+    def third(row, carry):
+        for f in range(2):
+            centre, total = shifted(u2, f, row + 1, 2 * G, size, first_, last_)
+            if f == 1:
+                total += jnp.where(first_, pltpu.roll(inj[1, G : G + size], 120 - row, 1), 0.0)
+            u3[f, row, yy] = (
+                abc[2, row + 1, yy] * centre
+                - abc[0, row + 1, yy] * u1[f, row + 2, yy]
+                + abc[1, row + 1, yy] * total
+            )
+        return carry
+
+    lax.fori_loop(0, 24, third, 0, unroll=12)
+    levels = ((u0, 9), (u1, 10), (u2, 9), (u3, 8))
+    groups = size // G
+    low = spot((start if first_slab else start - G), size, Y)
+
+    def out_copy(g):
+        return pltpu.make_async_copy(
+            image.at[:, :, pl.ds(by8(g * G), G)],
+            out_hbm.at[:, :, pl.ds(by8(low + g * G), G)],
+            out_sem.at[g],
+        )
+
+    def products(g, carry):
+        cells = pl.ds(by8(2 * G + g * G), G)
+        for parity in range(2):
+            for tile in range(3):
+                rows_a = [-8 + parity + 8 * tile + 2 * j for j in range(4)]
+                held = [[ref[0, a + o, cells] for ref, o in levels] for a in rows_a]
+                for b in range(-8 + parity, 16, 2):
+                    wanted = [
+                        j for j, a in enumerate(rows_a) if 0 <= a + b < 16 and abs(b - a) <= 16
+                    ]
+                    if not wanted:
+                        continue
+                    right = [ref[1, b + o, cells] for ref, o in levels]
+                    for j in wanted:
+                        a = rows_a[j]
+                        p = [l * r for l, r in zip(held[j], right)]
+                        image[(b - a) // 2 + 8, (a + b) // 2, pl.ds(by8(g * G), G)] = (
+                            p[0] + p[1]
+                        ) + (p[2] + p[3])
+        out_copy(g).start()
+        return carry
+
+    lax.fori_loop(0, groups, products, 0)
+    for g in range(groups):
+        out_copy(g).wait()
+
+
+def call(kernel, outs, args, specs, scratch, name, out_specs=None, **extra):
+    return pl.pallas_call(
+        kernel,
+        out_shape=[jax.ShapeDtypeStruct(s, F32) for s in outs],
+        in_specs=specs,
+        out_specs=out_specs or [HBM] * len(outs),
+        scratch_shapes=scratch,
+        compiler_params=pltpu.CompilerParams(vmem_limit_bytes=48 << 20),
+        name=name,
+        **extra,
+    )(*args)
+
+
+def shards(fields_now, fields_later, velocity_term, damping, traces, receiver_live):
+    count = lax.axis_size("gx")
+    swap_x = [(i, i ^ 1) for i in range(count)]
+    onward = [(i, i + 2) for i in range(0, count - 2, 2)]
+    onward += [(i, i - 2) for i in range(3, count, 2)]
+    backward = [(b, a) for a, b in onward]
+    swap = [(0, 1), (1, 0)]
+    dma = pltpu.SemaphoreType.DMA
+    vm = pltpu.VMEM
+    u0 = fields_now
+    small = [VMEM, VMEM]
+
+    edge, rest, mine, on0, brink = call(
+        prep_kernel,
+        [(2, 2, Y + G, Z), (2, 6, Y, Z), (X, Y, Z), (4, Y + G, Z), (2, X, G, Z)],
+        (u0, velocity_term, damping, traces, receiver_live),
+        [HBM] * 3 + small,
+        [vm((2, X, Y), F32), dma((12,))],
+        "prep",
+    )
+    near_edge = lax.ppermute(edge, "gx", swap_x)
+    beside = lax.ppermute(brink, "gy", swap)
+    near_mine = lax.ppermute(mine, "gx", swap_x)
+    near_rest = lax.ppermute(rest, "gx", swap_x)
+    from_on0 = lax.ppermute(on0, "gx", onward)
+    far_edge = lax.ppermute(near_edge, "gx", onward)
+
+    u1, on1, back, *parts = call(
+        functools.partial(first_kernel, CHUNKS),
+        [(2, X, Y, Z), (2, 2, Y, Z), (8, Y + G, Z)] + [(2, X, w, Z) for w in CHUNKS],
+        (u0, fields_later, velocity_term, damping, near_edge, far_edge, beside, traces,
+         receiver_live),
+        [HBM] * 7 + small,
+        [
+            vm((2, X + 2, Y + 2 * G, Z), F32),
+            vm((2, X, Y, Z), F32),
+            vm((X, Y, Z), F32),
+            vm((X, Y, Z), F32),
+            vm((2, X, Y, Z), F32),
+            vm((2, X, Y), F32),
+            dma((7 + len(CHUNKS),)),
+        ],
+        "first",
+    )
+    near_chunks = [lax.ppermute(p, "gx", swap_x) for p in parts]
+    from_back = lax.ppermute(back, "gx", backward)
+    from_on1 = lax.ppermute(on1, "gx", onward)
+    far_mine = lax.ppermute(near_mine, "gx", onward)
+    near_other = lax.ppermute(near_mine, "shot", swap)
+    far_other = lax.ppermute(far_mine, "shot", swap)
+    far_rest = lax.ppermute(near_rest, "gx", onward)
+    far_chunks = [lax.ppermute(c, "gx", onward) for c in near_chunks]
+
+    base0 = (
+        near_edge, near_rest, near_mine, near_other,
+        far_edge, far_rest, far_mine, far_other,
+        u0, velocity_term, damping, from_on0, from_back,
+    )
+    base1 = (u1, from_on1)
+    rim0, columns = call(
+        rim0_kernel,
+        [(106, G, Z), (2, Y, Z)],
+        (*base0, traces, receiver_live),
+        [HBM] * len(base0) + small,
+        [vm((2, 40, Y), F32), vm((2, 26, G, Z), F32), vm((2, 26, G, Z), F32), dma((25,))],
+        "rim0",
+        [VMEM, VMEM],
+    )
+    rim0 = lax.ppermute(rim0, "gy", swap)
+    (rim1,) = call(
+        functools.partial(rim1_kernel, CHUNKS[0]),
+        [(2, 28, G, Z)],
+        (*base1, from_back, near_chunks[0], far_chunks[0]),
+        [HBM] * 5,
+        [dma((6,))],
+        "rim1",
+        [VMEM],
+    )
+    rim1 = lax.ppermute(rim1, "gy", swap)
+
+    image = None
+    for k, width in enumerate(CHUNKS):
+        first_slab, last_slab = k == 0, k == len(CHUNKS) - 1
+        span = (G if first_slab else 2 * G) + width + (G if last_slab else 0)
+        args = [*base0, *base1, columns, near_chunks[k], far_chunks[k]]
+        if first_slab:
+            args += [rim0, rim1]
+        else:
+            args += [near_chunks[k - 1], far_chunks[k - 1], image]
+        wide = span + 2 * G
+        (image,) = call(
+            functools.partial(slab_kernel, k, CHUNKS),
+            [(2 * LAG_HALF + 1, X, Y, Z)],
+            args,
+            [HBM] * len(args),
+            [
+                vm((2, 26, wide, Z), F32),
+                vm((2, 28, wide, Z), F32),
+                vm((2, 26, wide, Z), F32),
+                vm((2, 24, wide, Z), F32),
+                vm((2, 26, wide, Z), F32),
+                vm((3, 26, wide, Z), F32),
+                vm((2, span, Z), F32),
+                vm((2 * LAG_HALF + 1, X, span - 2 * G, Z), F32),
+                dma((32,)),
+                dma((max(1, (span - 2 * G) // G),)),
+            ],
+            f"slab{k}",
+            input_output_aliases={} if first_slab else {len(args) - 1: 0},
+        )
+    return image
+
+
 def solution(mesh):
     placed = (
         P("shot", "gx", "gy", None),
@@ -79,6 +576,12 @@
         P("shot", "gx", "gy"),
         P("gx", "gy"),
     )
+
+    def body(fields_now, *others):
+        fits = fields_now.shape == (2, X, 128, 128) and mesh.shape["gx"] % 2 == 0
+        fits = fits and mesh.shape["gy"] == 2 and mesh.shape["shot"] == 2
+        return (shards if fits else plain)(fields_now, *others)
+
     return jax.shard_map(
-        shards, mesh=mesh, in_specs=placed, out_specs=P("shot", "gx", "gy", None), check_vma=False
-    )
+        body, mesh=mesh, in_specs=placed, out_specs=P("shot", "gx", "gy", None), check_vma=False
+    )

time: 216 us -> 117 us (0.54)
  the two profiles are of different devices: /device:TPU:25 before, /device:TPU:0 now
where the time goes in v1:
time: 117 us; the launch traced here: 116 us
  waiting for transfers between devices  45.9 us (39%)
  starting transfers between devices  37.9 us (32%)
  Pallas kernels  22.5 us (19%)
  local copies, waits for them, and re-layouts  9.07 us (8%)
    pallas_call x7, Pallas kernels, call(): pl.pallas_call(kernel, out_shape=[jax.ShapeDtypeStruct(s, F32) for s in o...  22.5 us
    ppermute x1, waiting for transfers between devices, shards(): near_edge = lax.ppermute(edge, 'gx', swap_x)  17.9 us
    ppermute x1, waiting for transfers between devices, shards(): near_mine = lax.ppermute(mine, 'gx', swap_x)  10.7 us
    ppermute x3, starting transfers between devices, shards(): far_chunks = [lax.ppermute(c, 'gx', onward) for c in near_chunks]  9.55 us
    unnamed x30, local copies, waits for them, and re-layouts  9.07 us
    ppermute x1, waiting for transfers between devices, shards(): near_other = lax.ppermute(near_mine, 'shot', swap)  5.67 us
    ppermute x3, waiting for transfers between devices, shards(): near_chunks = [lax.ppermute(p, 'gx', swap_x) for p in parts]  5.51 us
    ppermute x1, waiting for transfers between devices, shards(): far_other = lax.ppermute(far_mine, 'shot', swap)  4.56 us
  transfers between devices with their start and end apart: 20, of which 6 were waited for; matrix products, arithmetic and copies ran while one was open for 0% of the time, Pallas kernels for 14%

profile of v1, /device:TPU:0, one launch (start us, length us, event | category | flops | bytes accessed | tf_op | source)
XLA Modules:
  0.0 115.7 jit_solution(7275662562252327931)
XLA Ops:
  0.0 1.2 %copy-done = f32[2,8,128,128]{3,2,1,0:T(8,128)S(1)} copy-done((f32[2,8,128,128]{3,2,1,0:T(8,128)S(1)}, f32[2,8,128,128]{3,2,1,0:T(8,128)}, u32[]{:S(2)}) %copy-start) | copy-done | bytes 1048600
  1.2 1.0 copy-done.1
  2.3 1.0 copy-done.4
  3.3 0.7 copy-done.10
  4.0 0.7 copy-done.12
  4.7 0.7 prep.1
  5.4 3.0 %collective-permute-start.2 = (f32[8,128,128]{2,1,0:T(8,128)S(1)}, f32[8,128,128]{2,1,0:T(8,128)S(1)}, u32[]{:S(2)}, u32[]{:S(2)}) collective-permute-start(f32[8,128,128]{2,1,0:T(8,128)S(1)} %get-tuple-element.20), channel_id=1, source_target_pairs={{0,2},{2,0},{4,6},{6,4},{8,10},{10,8},{12,14},{14,12},{1,3},{3,1},... | collective-permute-start | bytes 1572872 | tf_op jit(solution)/shard_map/ppermute | solution.py:479
  8.4 0.1 collective-permute-start.1
  8.5 1.9 %collective-permute-start = (f32[2,2,136,128]{3,2,1,0:T(8,128)S(1)}, f32[2,2,136,128]{3,2,1,0:T(8,128)S(1)}, u32[]{:S(2)}, u32[]{:S(2)}) collective-permute-start(f32[2,2,136,128]{3,2,1,0:T(8,128)S(1)} %get-tuple-element.18), channel_id=1, source_target_pairs={{0,2},{2,0},{4,6},{6,4},{8,10},{10,8},{12,14},{14,12},{1,3},{3,1},... | collective-permute-start | bytes 835592 | tf_op jit(solution)/shard_map/ppermute | solution.py:477
  10.4 10.7 %collective-permute-done.2.args_2_ = f32[8,128,128]{2,1,0:T(8,128)S(1)} collective-permute-done((f32[8,128,128]{2,1,0:T(8,128)S(1)}, f32[8,128,128]{2,1,0:T(8,128)S(1)}, u32[]{:S(2)}, u32[]{:S(2)}) %collective-permute-start.2) | collective-permute-done | bytes 524320 | tf_op jit(solution)/shard_map/ppermute | solution.py:479
  21.1 4.1 %collective-permute-start.6 = (f32[8,128,128]{2,1,0:T(8,128)S(1)}, f32[8,128,128]{2,1,0:T(8,128)S(1)}, u32[]{:S(2)}, u32[]{:S(2)}) collective-permute-start(f32[8,128,128]{2,1,0:T(8,128)S(1)} %collective-permute-done.2.args_2_), channel_id=1, source_target_pairs={{0,4},{4,8},{8,12},{6,2},{10,6},{14,10},{1,5},{5,9},{9,13},{7,3},{... | collective-permute-start | bytes 1572872 | tf_op jit(solution)/shard_map/ppermute | solution.py:504
  25.2 17.9 %collective-permute-done.args_4_.args_0_ = f32[2,2,136,128]{3,2,1,0:T(8,128)S(1)} collective-permute-done((f32[2,2,136,128]{3,2,1,0:T(8,128)S(1)}, f32[2,2,136,128]{3,2,1,0:T(8,128)S(1)}, u32[]{:S(2)}, u32[]{:S(2)}) %collective-permute-start) | collective-permute-done | bytes 278560 | tf_op jit(solution)/shard_map/ppermute | solution.py:477
  43.1 3.7 %collective-permute-start.4 = (f32[2,2,136,128]{3,2,1,0:T(8,128)S(1)}, f32[2,2,136,128]{3,2,1,0:T(8,128)S(1)}, u32[]{:S(2)}, u32[]{:S(2)}) collective-permute-start(f32[2,2,136,128]{3,2,1,0:T(8,128)S(1)} %collective-permute-done.args_4_.args_0_), channel_id=1, source_target_pairs={{0,4},{4,8},{8,12},{6,2},{10,6},{14,10},{1,5},{5,9},{9,13},{7,3},{... | collective-permute-start | bytes 835592 | tf_op jit(solution)/shard_map/ppermute | solution.py:482
  46.9 3.5 %collective-permute-start.8 = (f32[4,136,128]{2,1,0:T(8,128)S(1)}, f32[4,136,128]{2,1,0:T(8,128)S(1)}, u32[]{:S(2)}, u32[]{:S(2)}) collective-permute-start(f32[4,136,128]{2,1,0:T(8,128)S(1)} %get-tuple-element.21), channel_id=1, source_target_pairs={{0,4},{4,8},{8,12},{6,2},{10,6},{14,10},{1,5},{5,9},{9,13},{7,3},{... | collective-permute-start | bytes 835592 | tf_op jit(solution)/shard_map/ppermute | solution.py:481
  50.4 0.1 collective-permute-start.9
  50.5 3.5 %collective-permute-start.5 = (f32[2,6,128,128]{3,2,1,0:T(8,128)S(1)}, f32[2,6,128,128]{3,2,1,0:T(8,128)S(1)}, u32[]{:S(2)}, u32[]{:S(2)}) collective-permute-start(f32[2,6,128,128]{3,2,1,0:T(8,128)S(1)} %collective-permute-done.1.args_1_), channel_id=1, source_target_pairs={{0,4},{4,8},{8,12},{6,2},{10,6},{14,10},{1,5},{5,9},{9,13},{7,3},{... | collective-permute-start | bytes 2359304 | tf_op jit(solution)/shard_map/ppermute | solution.py:507
  54.0 0.0 collective-permute-done.9.args_6_
  54.0 3.1 %first.1 = (f32[2,8,128,128]{3,2,1,0:T(8,128)S(1)}, f32[2,2,128,128]{3,2,1,0:T(8,128)S(1)}, f32[8,136,128]{2,1,0:T(8,128)S(1)}, f32[2,8,48,128]{3,2,1,0:T(8,128)...) custom-call(f32[2,8,128,128]{3,2,1,0:T(8,128)S(1)} %copy-done, f32[2,8,128,128]{3,2,1,0:T(8,128)} %args_1_.4, ...), custom_call_target="tpu_custom_call" | custom-call | tf_op jit(solution)/shard_map/first/pallas_call | solution.py:445
  57.2 2.4 %collective-permute-start.16 = (f32[2,8,48,128]{3,2,1,0:T(8,128)S(1)}, f32[2,8,48,128]{3,2,1,0:T(8,128)S(1)}, u32[]{:S(2)}, u32[]{:S(2)}) collective-permute-start(f32[2,8,48,128]{3,2,1,0:T(8,128)S(1)} %get-tuple-element.29), channel_id=1, source_target_pairs={{0,2},{2,0},{4,6},{6,4},{8,10},{10,8},{12,14},{14,12},{1,3},{3,1},... | collective-permute-start | bytes 1179656 | tf_op jit(solution)/shard_map/ppermute | solution.py:501
  59.5 1.5 %collective-permute-start.3 = (f32[8,128,128]{2,1,0:T(8,128)S(1)}, f32[8,128,128]{2,1,0:T(8,128)S(1)}, u32[]{:S(2)}, u32[]{:S(2)}) collective-permute-start(f32[8,128,128]{2,1,0:T(8,128)S(1)} %collective-permute-done.2.args_2_), channel_id=1, source_target_pairs={{0,16},{16,0},{1,17},{17,1},{2,18},{18,2},{3,19},{19,3},{4,20},{20... | collective-permute-start | bytes 1572872 | tf_op jit(solution)/shard_map/ppermute | solution.py:505
  61.0 1.3 %collective-permute-start.10 = (f32[8,136,128]{2,1,0:T(8,128)S(1)}, f32[8,136,128]{2,1,0:T(8,128)S(1)}, u32[]{:S(2)}, u32[]{:S(2)}) collective-permute-start(f32[8,136,128]{2,1,0:T(8,128)S(1)} %get-tuple-element.23), channel_id=1, source_target_pairs={{4,0},{8,4},{12,8},{2,6},{6,10},{10,14},{5,1},{9,5},{13,9},{3,7},{... | collective-permute-start | bytes 1671176 | tf_op jit(solution)/shard_map/ppermute | solution.py:502
  62.3 0.0 collective-permute-done.6.args_6_
  62.3 0.6 collective-permute-start.7
  62.9 5.5 %collective-permute-done.16.args_3_.args_16_.args_18_ = f32[2,8,48,128]{3,2,1,0:T(8,128)S(1)} collective-permute-done((f32[2,8,48,128]{3,2,1,0:T(8,128)S(1)}, f32[2,8,48,128]{3,2,1,0:T(8,128)S(1)}, u32[]{:S(2)}, u32[]{:S(2)}) %collective-permute-start.16) | collective-permute-done | bytes 393248 | tf_op jit(solution)/shard_map/ppermute | solution.py:501
  68.4 0.3 collective-permute-start.14
  68.7 5.7 %collective-permute-done.3.args_3_ = f32[8,128,128]{2,1,0:T(8,128)S(1)} collective-permute-done((f32[8,128,128]{2,1,0:T(8,128)S(1)}, f32[8,128,128]{2,1,0:T(8,128)S(1)}, u32[]{:S(2)}, u32[]{:S(2)}) %collective-permute-start.3) | collective-permute-done | bytes 524320 | tf_op jit(solution)/shard_map/ppermute | solution.py:505
  74.4 3.5 %collective-permute-start.17 = (f32[2,8,48,128]{3,2,1,0:T(8,128)S(1)}, f32[2,8,48,128]{3,2,1,0:T(8,128)S(1)}, u32[]{:S(2)}, u32[]{:S(2)}) collective-permute-start(f32[2,8,48,128]{3,2,1,0:T(8,128)S(1)} %collective-permute-done.16.args_3_.args_16_.args_18_), channel_id=1, source_target_pairs={{0,4},{4,8},{8,12},{6,2},{10,6},{14,10},{1,5},{5,9},{9,13},{7,3},{... | collective-permute-start | bytes 1179656 | tf_op jit(solution)/shard_map/ppermute | solution.py:508
  77.9 0.0 collective-permute-done.10.args_12_.args_2_
  77.9 0.1 collective-permute-start.12
  78.0 4.6 %collective-permute-done.7.args_7_ = f32[8,128,128]{2,1,0:T(8,128)S(1)} collective-permute-done((f32[8,128,128]{2,1,0:T(8,128)S(1)}, f32[8,128,128]{2,1,0:T(8,128)S(1)}, u32[]{:S(2)}, u32[]{:S(2)}) %collective-permute-start.7) | collective-permute-done | bytes 524320 | tf_op jit(solution)/shard_map/ppermute | solution.py:506
  82.6 2.2 %collective-permute-start.11 = (f32[2,2,128,128]{3,2,1,0:T(8,128)S(1)}, f32[2,2,128,128]{3,2,1,0:T(8,128)S(1)}, u32[]{:S(2)}, u32[]{:S(2)}) collective-permute-start(f32[2,2,128,128]{3,2,1,0:T(8,128)S(1)} %get-tuple-element.25), channel_id=1, source_target_pairs={{0,4},{4,8},{8,12},{6,2},{10,6},{14,10},{1,5},{5,9},{9,13},{7,3},{... | collective-permute-start | bytes 786440 | tf_op jit(solution)/shard_map/ppermute | solution.py:503
  84.7 0.0 collective-permute-done.5.args_5_
  84.7 0.9 copy-done.14
  85.6 1.0 copy-done.2
  86.7 1.0 copy-done.5
  87.7 0.7 copy-done.11
  88.4 0.7 copy-done.13
  89.1 1.3 %rim0.1 = (f32[106,8,128]{2,1,0:T(8,128)S(1)}, f32[2,128,128]{2,1,0:T(8,128)S(1)}) custom-call(f32[2,2,136,128]{3,2,1,0:T(8,128)S(1)} %collective-permute-done.args_4_.args_0_, f32[2,6,128,128]{3,2,1,0:T(8,128)S(1)} %collective-permute-done.1.args_1_, f32[8,128,128]{2,1,0:T(8,128)S(1)} %collective-permute-done.2.args_2_, ...), custom_call_target="tpu_custom_call" | custom-call | tf_op jit(solution)/shard_map/rim0/pallas_call | solution.py:445
  90.4 0.1 collective-permute-start.18
  90.5 0.0 collective-permute-done.14.args_16_.args_18_
  90.5 2.6 %collective-permute-start.15 = (f32[2,8,48,128]{3,2,1,0:T(8,128)S(1)}, f32[2,8,48,128]{3,2,1,0:T(8,128)S(1)}, u32[]{:S(2)}, u32[]{:S(2)}) collective-permute-start(f32[2,8,48,128]{3,2,1,0:T(8,128)S(1)} %collective-permute-done.14.args_16_.args_18_), channel_id=1, source_target_pairs={{0,4},{4,8},{8,12},{6,2},{10,6},{14,10},{1,5},{5,9},{9,13},{7,3},{... | collective-permute-start | bytes 1179656 | tf_op jit(solution)/shard_map/ppermute | solution.py:508
  93.0 3.5 %collective-permute-start.13 = (f32[2,8,32,128]{3,2,1,0:T(8,128)S(1)}, f32[2,8,32,128]{3,2,1,0:T(8,128)S(1)}, u32[]{:S(2)}, u32[]{:S(2)}) collective-permute-start(f32[2,8,32,128]{3,2,1,0:T(8,128)S(1)} %collective-permute-done.12.args_16_), channel_id=1, source_target_pairs={{0,4},{4,8},{8,12},{6,2},{10,6},{14,10},{1,5},{5,9},{9,13},{7,3},{... | collective-permute-start | bytes 786440 | tf_op jit(solution)/shard_map/ppermute | solution.py:508
  96.6 0.1 rim1.1
  96.7 0.1 collective-permute-start.19
  96.8 1.5 %collective-permute-done.19.args_19_ = f32[2,28,8,128]{3,2,1,0:T(8,128)S(1)} collective-permute-done((f32[2,28,8,128]{3,2,1,0:T(8,128)S(1)}, f32[2,28,8,128]{3,2,1,0:T(8,128)S(1)}, u32[]{:S(2)}, u32[]{:S(2)}) %collective-permute-start.19) | collective-permute-done | bytes 229408 | tf_op jit(solution)/shard_map/ppermute | solution.py:535
  98.3 5.6 %slab0.1.args_20_ = f32[17,8,128,128]{3,2,1,0:T(8,128)} custom-call(f32[2,2,136,128]{3,2,1,0:T(8,128)S(1)} %collective-permute-done.args_4_.args_0_, f32[2,6,128,128]{3,2,1,0:T(8,128)} %copy-done.9, f32[8,128,128]{2,1,0:T(8,128)S(1)} %collective-permute-done.2.args_2_, f32[8,128,128]{2,1,0:T(8,128)S(1)} %collective-permute-done.3.args_3_, ...), custom_call_target="tpu_custom_call" | custom-call | tf_op jit(solution)/shard_map/slab0/pallas_call | solution.py:445
  103.9 6.2 %slab1.1.args_20_ = f32[17,8,128,128]{3,2,1,0:T(8,128)} custom-call(f32[2,2,136,128]{3,2,1,0:T(8,128)S(1)} %collective-permute-done.args_4_.args_0_, f32[2,6,128,128]{3,2,1,0:T(8,128)} %copy-done.9, f32[8,128,128]{2,1,0:T(8,128)S(1)} %collective-permute-done.2.args_2_, ...), custom_call_target="tpu_custom_call", output_to_operand_aliasing={{}: (20, {})} | custom-call | tf_op jit(solution)/shard_map/slab1/pallas_call | solution.py:445
  110.1 5.6 %slab2.1 = f32[17,8,128,128]{3,2,1,0:T(8,128)} custom-call(f32[2,2,136,128]{3,2,1,0:T(8,128)S(1)} %collective-permute-done.args_4_.args_0_, f32[2,6,128,128]{3,2,1,0:T(8,128)} %copy-done.9, f32[8,128,128]{2,1,0:T(8,128)S(1)} %collective-permute-done.2.args_2_, f32[8,128,128]{2,1,0:T(8,128)S(1)} %collective-permute-done.3.args_3_, ...), custom_call_target="tpu_custom_call", output_to_operand_aliasing={{}: (20, {})} | custom-call | tf_op jit(solution)/shard_map/slab2/pallas_call | solution.py:445
  (29 shorter events, 0.1 us)
Async XLA Ops:
  0.0 1.2 %copy-start = (f32[2,8,128,128]{3,2,1,0:T(8,128)S(1)}, f32[2,8,128,128]{3,2,1,0:T(8,128)}, u32[]{:S(2)}) copy-start(f32[2,8,128,128]{3,2,1,0:T(8,128)} %args_8_.9) | copy-start | bytes 3145732
  1.2 1.0 copy-start.1
  2.3 1.0 copy-start.4
  3.3 0.7 copy-start.10
  4.0 0.7 copy-start.12
  4.7 93.6 %copy-start.3 = (f32[8,128,128]{2,1,0:T(8,128)S(1)}, f32[8,128,128]{2,1,0:T(8,128)}, u32[]{:S(2)}) copy-start(f32[8,128,128]{2,1,0:T(8,128)} %args_9_.7) | copy-start | bytes 1572868
  4.7 93.6 %copy-start.6 = (f32[8,128,128]{2,1,0:T(8,128)S(1)}, f32[8,128,128]{2,1,0:T(8,128)}, u32[]{:S(2)}) copy-start(f32[8,128,128]{2,1,0:T(8,128)} %args_10_.7) | copy-start | bytes 1572868
  5.4 15.8 %collective-permute-start.2 = (f32[8,128,128]{2,1,0:T(8,128)S(1)}, f32[8,128,128]{2,1,0:T(8,128)S(1)}, u32[]{:S(2)}, u32[]{:S(2)}) collective-permute-start(f32[8,128,128]{2,1,0:T(8,128)S(1)} %get-tuple-element.20), channel_id=1, source_target_pairs={{0,2},{2,0},{4,6},{6,4},{8,10},{10,8},{12,14},{14,12},{1,3},{3,1},... | collective-permute-start | bytes 1572872 | tf_op jit(solution)/shard_map/ppermute | solution.py:479
  8.4 42.1 %collective-permute-start.1 = (f32[2,6,128,128]{3,2,1,0:T(8,128)S(1)}, f32[2,6,128,128]{3,2,1,0:T(8,128)S(1)}, u32[]{:S(2)}, u32[]{:S(2)}) collective-permute-start(f32[2,6,128,128]{3,2,1,0:T(8,128)S(1)} %get-tuple-element.19), channel_id=1, source_target_pairs={{0,2},{2,0},{4,6},{6,4},{8,10},{10,8},{12,14},{14,12},{1,3},{3,1},... | collective-permute-start | bytes 2359304 | tf_op jit(solution)/shard_map/ppermute | solution.py:480
  8.5 34.7 %collective-permute-start = (f32[2,2,136,128]{3,2,1,0:T(8,128)S(1)}, f32[2,2,136,128]{3,2,1,0:T(8,128)S(1)}, u32[]{:S(2)}, u32[]{:S(2)}) collective-permute-start(f32[2,2,136,128]{3,2,1,0:T(8,128)S(1)} %get-tuple-element.18), channel_id=1, source_target_pairs={{0,2},{2,0},{4,6},{6,4},{8,10},{10,8},{12,14},{14,12},{1,3},{3,1},... | collective-permute-start | bytes 835592 | tf_op jit(solution)/shard_map/ppermute | solution.py:477
  21.1 41.2 %collective-permute-start.6 = (f32[8,128,128]{2,1,0:T(8,128)S(1)}, f32[8,128,128]{2,1,0:T(8,128)S(1)}, u32[]{:S(2)}, u32[]{:S(2)}) collective-permute-start(f32[8,128,128]{2,1,0:T(8,128)S(1)} %collective-permute-done.2.args_2_), channel_id=1, source_target_pairs={{0,4},{4,8},{8,12},{6,2},{10,6},{14,10},{1,5},{5,9},{9,13},{7,3},{... | collective-permute-start | bytes 1572872 | tf_op jit(solution)/shard_map/ppermute | solution.py:504
  43.1 10.9 %collective-permute-start.4 = (f32[2,2,136,128]{3,2,1,0:T(8,128)S(1)}, f32[2,2,136,128]{3,2,1,0:T(8,128)S(1)}, u32[]{:S(2)}, u32[]{:S(2)}) collective-permute-start(f32[2,2,136,128]{3,2,1,0:T(8,128)S(1)} %collective-permute-done.args_4_.args_0_), channel_id=1, source_target_pairs={{0,4},{4,8},{8,12},{6,2},{10,6},{14,10},{1,5},{5,9},{9,13},{7,3},{... | collective-permute-start | bytes 835592 | tf_op jit(solution)/shard_map/ppermute | solution.py:482
  46.9 14.2 %collective-permute-start.8 = (f32[4,136,128]{2,1,0:T(8,128)S(1)}, f32[4,136,128]{2,1,0:T(8,128)S(1)}, u32[]{:S(2)}, u32[]{:S(2)}) collective-permute-start(f32[4,136,128]{2,1,0:T(8,128)S(1)} %get-tuple-element.21), channel_id=1, source_target_pairs={{0,4},{4,8},{8,12},{6,2},{10,6},{14,10},{1,5},{5,9},{9,13},{7,3},{... | collective-permute-start | bytes 835592 | tf_op jit(solution)/shard_map/ppermute | solution.py:481
  50.4 3.6 %collective-permute-start.9 = (f32[2,8,8,128]{3,2,1,0:T(8,128)S(1)}, f32[2,8,8,128]{3,2,1,0:T(8,128)S(1)}, u32[]{:S(2)}, u32[]{:S(2)}) collective-permute-start(f32[2,8,8,128]{3,2,1,0:T(8,128)S(1)} %get-tuple-element.22), channel_id=1, source_target_pairs={{0,1},{1,0},{2,3},{3,2},{4,5},{5,4},{6,7},{7,6},{8,9},{9,8},{10,11... | collective-permute-start | bytes 196616 | tf_op jit(solution)/shard_map/ppermute | solution.py:478
  50.5 47.8 %copy-start.9 = (f32[2,6,128,128]{3,2,1,0:T(8,128)}, f32[2,6,128,128]{3,2,1,0:T(8,128)S(1)}, u32[]{:S(2)}) copy-start(f32[2,6,128,128]{3,2,1,0:T(8,128)S(1)} %collective-permute-done.1.args_1_) | copy-start | bytes 2359300
  50.5 34.2 %collective-permute-start.5 = (f32[2,6,128,128]{3,2,1,0:T(8,128)S(1)}, f32[2,6,128,128]{3,2,1,0:T(8,128)S(1)}, u32[]{:S(2)}, u32[]{:S(2)}) collective-permute-start(f32[2,6,128,128]{3,2,1,0:T(8,128)S(1)} %collective-permute-done.1.args_1_), channel_id=1, source_target_pairs={{0,4},{4,8},{8,12},{6,2},{10,6},{14,10},{1,5},{5,9},{9,13},{7,3},{... | collective-permute-start | bytes 2359304 | tf_op jit(solution)/shard_map/ppermute | solution.py:507
  57.1 41.1 %copy-start.7 = (f32[2,8,128,128]{3,2,1,0:T(8,128)}, f32[2,8,128,128]{3,2,1,0:T(8,128)S(1)}, u32[]{:S(2)}) copy-start(f32[2,8,128,128]{3,2,1,0:T(8,128)S(1)} %get-tuple-element.24.args_0_.args_13_) | copy-start | bytes 3145732
  57.2 11.3 %collective-permute-start.16 = (f32[2,8,48,128]{3,2,1,0:T(8,128)S(1)}, f32[2,8,48,128]{3,2,1,0:T(8,128)S(1)}, u32[]{:S(2)}, u32[]{:S(2)}) collective-permute-start(f32[2,8,48,128]{3,2,1,0:T(8,128)S(1)} %get-tuple-element.29), channel_id=1, source_target_pairs={{0,2},{2,0},{4,6},{6,4},{8,10},{10,8},{12,14},{14,12},{1,3},{3,1},... | collective-permute-start | bytes 1179656 | tf_op jit(solution)/shard_map/ppermute | solution.py:501
  59.5 14.9 %collective-permute-start.3 = (f32[8,128,128]{2,1,0:T(8,128)S(1)}, f32[8,128,128]{2,1,0:T(8,128)S(1)}, u32[]{:S(2)}, u32[]{:S(2)}) collective-permute-start(f32[8,128,128]{2,1,0:T(8,128)S(1)} %collective-permute-done.2.args_2_), channel_id=1, source_target_pairs={{0,16},{16,0},{1,17},{17,1},{2,18},{18,2},{3,19},{19,3},{4,20},{20... | collective-permute-start | bytes 1572872 | tf_op jit(solution)/shard_map/ppermute | solution.py:505
  61.0 16.8 %collective-permute-start.10 = (f32[8,136,128]{2,1,0:T(8,128)S(1)}, f32[8,136,128]{2,1,0:T(8,128)S(1)}, u32[]{:S(2)}, u32[]{:S(2)}) collective-permute-start(f32[8,136,128]{2,1,0:T(8,128)S(1)} %get-tuple-element.23), channel_id=1, source_target_pairs={{4,0},{8,4},{12,8},{2,6},{6,10},{10,14},{5,1},{9,5},{13,9},{3,7},{... | collective-permute-start | bytes 1671176 | tf_op jit(solution)/shard_map/ppermute | solution.py:502
  62.3 20.2 %collective-permute-start.7 = (f32[8,128,128]{2,1,0:T(8,128)S(1)}, f32[8,128,128]{2,1,0:T(8,128)S(1)}, u32[]{:S(2)}, u32[]{:S(2)}) collective-permute-start(f32[8,128,128]{2,1,0:T(8,128)S(1)} %collective-permute-done.6.args_6_), channel_id=1, source_target_pairs={{0,16},{16,0},{1,17},{17,1},{2,18},{18,2},{3,19},{19,3},{4,20},{20... | collective-permute-start | bytes 1572872 | tf_op jit(solution)/shard_map/ppermute | solution.py:506
  68.4 22.0 %collective-permute-start.14 = (f32[2,8,48,128]{3,2,1,0:T(8,128)S(1)}, f32[2,8,48,128]{3,2,1,0:T(8,128)S(1)}, u32[]{:S(2)}, u32[]{:S(2)}) collective-permute-start(f32[2,8,48,128]{3,2,1,0:T(8,128)S(1)} %get-tuple-element.28), channel_id=1, source_target_pairs={{0,2},{2,0},{4,6},{6,4},{8,10},{10,8},{12,14},{14,12},{1,3},{3,1},... | collective-permute-start | bytes 1179656 | tf_op jit(solution)/shard_map/ppermute | solution.py:501
  74.4 22.2 %collective-permute-start.17 = (f32[2,8,48,128]{3,2,1,0:T(8,128)S(1)}, f32[2,8,48,128]{3,2,1,0:T(8,128)S(1)}, u32[]{:S(2)}, u32[]{:S(2)}) collective-permute-start(f32[2,8,48,128]{3,2,1,0:T(8,128)S(1)} %collective-permute-done.16.args_3_.args_16_.args_18_), channel_id=1, source_target_pairs={{0,4},{4,8},{8,12},{6,2},{10,6},{14,10},{1,5},{5,9},{9,13},{7,3},{... | collective-permute-start | bytes 1179656 | tf_op jit(solution)/shard_map/ppermute | solution.py:508
  77.9 20.4 %copy-start.8 = (f32[8,136,128]{2,1,0:T(8,128)}, f32[8,136,128]{2,1,0:T(8,128)S(1)}, u32[]{:S(2)}) copy-start(f32[8,136,128]{2,1,0:T(8,128)S(1)} %collective-permute-done.10.args_12_.args_2_) | copy-start | bytes 1671172
  77.9 15.1 %collective-permute-start.12 = (f32[2,8,32,128]{3,2,1,0:T(8,128)S(1)}, f32[2,8,32,128]{3,2,1,0:T(8,128)S(1)}, u32[]{:S(2)}, u32[]{:S(2)}) collective-permute-start(f32[2,8,32,128]{3,2,1,0:T(8,128)S(1)} %get-tuple-element.27), channel_id=1, source_target_pairs={{0,2},{2,0},{4,6},{6,4},{8,10},{10,8},{12,14},{14,12},{1,3},{3,1},... | collective-permute-start | bytes 786440 | tf_op jit(solution)/shard_map/ppermute | solution.py:501
  82.6 14.0 %collective-permute-start.11 = (f32[2,2,128,128]{3,2,1,0:T(8,128)S(1)}, f32[2,2,128,128]{3,2,1,0:T(8,128)S(1)}, u32[]{:S(2)}, u32[]{:S(2)}) collective-permute-start(f32[2,2,128,128]{3,2,1,0:T(8,128)S(1)} %get-tuple-element.25), channel_id=1, source_target_pairs={{0,4},{4,8},{8,12},{6,2},{10,6},{14,10},{1,5},{5,9},{9,13},{7,3},{... | collective-permute-start | bytes 786440 | tf_op jit(solution)/shard_map/ppermute | solution.py:503
  84.7 0.9 copy-start.14
  85.6 1.0 copy-start.2
  86.7 1.0 copy-start.5
  87.7 0.7 copy-start.11
  88.4 0.7 copy-start.13
  90.4 7.9 %collective-permute-start.18 = (f32[106,8,128]{2,1,0:T(8,128)S(1)}, f32[106,8,128]{2,1,0:T(8,128)S(1)}, u32[]{:S(2)}, u32[]{:S(2)}) collective-permute-start(f32[106,8,128]{2,1,0:T(8,128)S(1)} %get-tuple-element.30), channel_id=1, source_target_pairs={{0,1},{1,0},{2,3},{3,2},{4,5},{5,4},{6,7},{7,6},{8,9},{9,8},{10,11... | collective-permute-start | bytes 1302536 | tf_op jit(solution)/shard_map/ppermute | solution.py:525
  90.5 13.4 %collective-permute-start.15 = (f32[2,8,48,128]{3,2,1,0:T(8,128)S(1)}, f32[2,8,48,128]{3,2,1,0:T(8,128)S(1)}, u32[]{:S(2)}, u32[]{:S(2)}) collective-permute-start(f32[2,8,48,128]{3,2,1,0:T(8,128)S(1)} %collective-permute-done.14.args_16_.args_18_), channel_id=1, source_target_pairs={{0,4},{4,8},{8,12},{6,2},{10,6},{14,10},{1,5},{5,9},{9,13},{7,3},{... | collective-permute-start | bytes 1179656 | tf_op jit(solution)/shard_map/ppermute | solution.py:508
  93.0 17.0 %collective-permute-start.13 = (f32[2,8,32,128]{3,2,1,0:T(8,128)S(1)}, f32[2,8,32,128]{3,2,1,0:T(8,128)S(1)}, u32[]{:S(2)}, u32[]{:S(2)}) collective-permute-start(f32[2,8,32,128]{3,2,1,0:T(8,128)S(1)} %collective-permute-done.12.args_16_), channel_id=1, source_target_pairs={{0,4},{4,8},{8,12},{6,2},{10,6},{14,10},{1,5},{5,9},{9,13},{7,3},{... | collective-permute-start | bytes 786440 | tf_op jit(solution)/shard_map/ppermute | solution.py:508
  96.7 1.6 %collective-permute-start.19 = (f32[2,28,8,128]{3,2,1,0:T(8,128)S(1)}, f32[2,28,8,128]{3,2,1,0:T(8,128)S(1)}, u32[]{:S(2)}, u32[]{:S(2)}) collective-permute-start(f32[2,28,8,128]{3,2,1,0:T(8,128)S(1)} %rim1.1), channel_id=1, source_target_pairs={{0,1},{1,0},{2,3},{3,2},{4,5},{5,4},{6,7},{7,6},{8,9},{9,8},{10,11... | collective-permute-start | bytes 688136 | tf_op jit(solution)/shard_map/ppermute | solution.py:535

commit v2 on v1

v2 whole, which is shorter than its diff:
```python
import functools
import jax
import jax.numpy as jnp
from jax import lax
from jax.experimental import pallas as pl
from jax.experimental.pallas import tpu as pltpu
from jax.sharding import PartitionSpec as P

STEPS = 4
LAG_HALF = 8
CHUNKS = (64, 64)


def padded(cells, sides, width):
    for axis, dim in sides:
        count = lax.axis_size(axis)
        ends = count - 1
        head = lax.slice_in_dim(cells, 0, width, axis=dim)
        tail = lax.slice_in_dim(cells, cells.shape[dim] - width, cells.shape[dim], axis=dim)
        cells = jnp.concatenate(
            [
                lax.ppermute(tail, axis, [(i, (i + 1) % count) for i in range(ends)]),
                cells,
                lax.ppermute(head, axis, [((i + 1) % count, i) for i in range(ends)]),
            ],
            axis=dim,
        )
    return cells


def lag_products(image_lags, slab, start, cells_x):
    updated = []
    for index, offset in enumerate(range(-LAG_HALF, LAG_HALF + 1)):
        left = slab[0, start - offset : start - offset + cells_x]
        right = slab[1, start + offset : start + offset + cells_x]
        updated.append(image_lags[index] + left * right)
    return updated


def source_mask(shape):
    channel_pick = (lax.broadcasted_iota(jnp.int32, shape, 0) == 1).astype(jnp.float32)
    surface = (lax.broadcasted_iota(jnp.int32, shape, 3) == 0).astype(jnp.float32)
    return channel_pick * surface


def plain(fields_now, fields_later, velocity_term, damping, traces, receiver_live):
    cells_x = fields_now.shape[1]
    live_mask = receiver_live.astype(jnp.float32)
    image_lags = [
        jnp.zeros(fields_now.shape[1:], jnp.float32) for offset in range(2 * LAG_HALF + 1)
    ]
    current = fields_now
    following = fields_later
    inject = source_mask(fields_now.shape)
    for time_step in range(STEPS):
        extended = padded(current, (("gx", 1),), LAG_HALF)
        image_lags = lag_products(image_lags, extended, LAG_HALF, cells_x)
        if time_step < STEPS - 1:
            crossed = padded(current, (("gy", 2),), 1)
            sum_x = (
                extended[:, LAG_HALF + 1 : LAG_HALF + 1 + cells_x]
                + extended[:, LAG_HALF - 1 : LAG_HALF - 1 + cells_x]
            )
            sum_y = crossed[:, :, 2:] + crossed[:, :, :-2]
            depth_pad = jnp.pad(current, ((0, 0), (0, 0), (0, 0), (1, 1)))
            sum_z = depth_pad[:, :, :, 2:] + depth_pad[:, :, :, :-2]
            source_plane = (live_mask * traces[time_step])[None, :, :, None]
            operated = sum_x + sum_y + sum_z - 6.0 * current + inject * source_plane
            earlier = (2.0 * current - (1.0 - damping) * following + velocity_term * operated) / (
                1.0 + damping
            )
            following = current
            current = earlier
    return jnp.stack(image_lags)


PARTS = 5
X = 8
Y = 128
Z = 128
G = 8
F32 = jnp.float32
HBM = pl.BlockSpec(memory_space=pltpu.HBM)
VMEM = pl.BlockSpec(memory_space=pltpu.VMEM)


def by8(value):
    return pl.multiple_of(value, G)


def place():
    even = lax.axis_index("gx") % 2 == 0
    return even, lax.axis_index("gy"), lax.axis_index("shot")


def run_copies(pieces, sem):
    copies = [pltpu.make_async_copy(a, b, sem.at[j]) for j, (a, b) in enumerate(pieces)]
    for c in copies:
        c.start()
    return copies


def wait_all(copies):
    for c in copies:
        c.wait()


def shifted(ref, f, row, lo, size, first, last):
    centre = ref[f, row, lo : lo + size]
    total = ref[f, row - 1, lo : lo + size] + ref[f, row + 1, lo : lo + size]
    total += ref[f, row, lo - 1 : lo - 1 + size] + ref[f, row, lo + 1 : lo + 1 + size]
    total += jnp.where(first, 0.0, pltpu.roll(centre, 1, 1))
    total += jnp.where(last, 0.0, pltpu.roll(centre, Z - 1, 1))
    return centre, total


def coefficients(vel, damp):
    inv = 1.0 / (1.0 + damp)
    gain = vel * inv
    return (1.0 - damp) * inv, gain, 2.0 * inv - 6.0 * gain


def receivers(traces_hbm, live_hbm, traces, live, sem):
    copies = run_copies([(traces_hbm, traces), (live_hbm, live)], sem)
    wait_all(copies)
    return live[...].astype(F32)


def edge_kernel(u0, edge, brink, sem):
    even, gy, shot = place()
    y = by8(jnp.where(gy == 0, Y - G, 0))
    pieces = [(u0.at[:, r], edge.at[:, e]) for e, r in ((0, 0), (1, X - 1))]
    pieces.append((u0.at[:, :, pl.ds(y, G)], brink))
    wait_all(run_copies(pieces, sem))


def prep_kernel(u0, v, d, traces_hbm, live_hbm, mine, rest, on0, back0, *scratch):
    t, traces, live, sem, sem2 = scratch
    even, gy, shot = place()
    own = pl.ds(0, Y)
    row = jnp.where(even, X - 1, 0)

    @pl.when(shot == 0)
    def _():
        pltpu.make_async_copy(v, mine.at[:, own], sem.at[7]).start()

    @pl.when(shot != 0)
    def _():
        pltpu.make_async_copy(d, mine.at[:, own], sem.at[7]).start()

    pieces = [(u0.at[:, pl.ds(1, 6)], rest)]
    for part, r in ((on0, row), (back0, X - 1 - row)):
        pieces.append((u0.at[:, r], part.at[pl.ds(0, 2), own]))
        pieces.append((v.at[r], part.at[2, own]))
        pieces.append((d.at[r], part.at[3, own]))
    copies = run_copies(pieces, sem)
    mask = receivers(traces_hbm, live_hbm, traces, live, sem2)
    for n in range(2):
        t[n] = mask * traces[n + 1]
    late = []
    for n in range(2):
        for k, part in enumerate((mine, on0, back0)):
            c = pltpu.make_async_copy(t.at[n], part.at[n, pl.ds(Y, G)], sem2.at[2 + 2 * k + n])
            c.start()
            late.append(c)
    wait_all(copies + late)
    pltpu.make_async_copy(v, mine.at[:, own], sem.at[7]).wait()


def surface_columns(rows):
    wide = jnp.concatenate([rows, jnp.zeros((Z - rows.shape[0], Y), F32)], 0)
    return wide.T


def first_kernel(chunks, *args):
    u0, later, v, d, near_e, far_e, beside, traces_hbm, live_hbm = args[:9]
    u1, on1, brow = args[9:12]
    parts = args[12 : 12 + len(chunks)]
    c, f0, vel, damp, out, traces, live, sem, sem2 = args[12 + len(chunks) :]
    even, gy, shot = place()
    own = pl.ds(0, Y)
    near_pick, near_row = jnp.where(even, 0, 1), jnp.where(even, 9, 0)
    far_pick, far_row = jnp.where(even, 1, 0), jnp.where(even, 0, 9)
    mid = pl.ds(G, Y)
    at = by8(jnp.where(gy == 0, Y + G, 0))
    copies = run_copies(
        [
            (u0, c.at[:, pl.ds(1, X), mid]),
            (near_e.at[:, near_pick], c.at[:, near_row, mid]),
            (far_e.at[:, far_pick], c.at[:, far_row, mid]),
            (beside, c.at[:, pl.ds(1, X), pl.ds(at, G)]),
            (later, f0),
            (v, vel),
            (d, damp),
        ],
        sem,
    )
    rim = by8(jnp.where(gy == 0, 0, Y + G))
    for f in range(2):
        for x in range(X):
            c[f, x + 1, pl.ds(rim, G)] = jnp.zeros((G, Z), F32)
    mask = receivers(traces_hbm, live_hbm, traces, live, sem2)
    column = surface_columns(mask * traces[0])
    wait_all(copies)
    lane = lax.broadcasted_iota(jnp.int32, (Y, Z), 1)
    first, last = lane == 0, lane == Z - 1
    for x in range(X):
        pull, gain, keep = coefficients(vel[x], damp[x])
        for f in range(2):
            centre, total = shifted(c, f, x + 1, G, Y, first, last)
            if f == 1:
                turned = pltpu.roll(column, Z - x, 1) if x else column
                total += jnp.where(first, turned, 0.0)
            out[f, x] = keep * centre - pull * f0[f, x] + gain * total
    row = jnp.where(even, 0, 6)
    pieces = [(out, u1), (out.at[:, pl.ds(6 - row, 2)], on1), (out.at[:, pl.ds(row, 2)], brow)]
    others = pl.ds(jnp.where(even, 2, 0), 6)
    begin = 0
    for width, part in zip(chunks, parts):
        y = by8(jnp.where(gy == 1, begin, Y - begin - width))
        pieces.append((out.at[:, others, pl.ds(y, width)], part))
        begin += width
    wait_all(run_copies(pieces, sem))


NAMES0 = ("ne", "nr", "na", "nb", "fe", "fr", "fa", "fb", "u0", "v", "d", "on", "back")
NAMES1 = ("u1", "on1", "back1", "nw", "fw")


def level0_pieces(refs, u0, co, src, dst, size, even, shot):
    near, far = jnp.where(even, 17, 1), jnp.where(even, 1, 17)
    s, d = pl.ds(src, size), pl.ds(dst, size)
    early, late = [], []
    for out, base, edge, rest, mine, other in (
        (early, near, refs["ne"], refs["nr"], refs["na"], refs["nb"]),
        (late, far, refs["fe"], refs["fr"], refs["fa"], refs["fb"]),
    ):
        out.append((edge.at[:, 0, s], u0(base, None, d)))
        out.append((edge.at[:, 1, s], u0(base + 7, None, d)))
        out.append((rest.at[:, :, s], u0(base + 1, 6, d)))
        out.append((mine.at[:, s], co(base, X, d, shot)))
        out.append((other.at[:, s], co(base, X, d, 1 - shot)))
    early.append((refs["u0"].at[:, :, s], u0(9, X, d)))
    early.append((refs["v"].at[:, s], co(9, X, d, 0)))
    early.append((refs["d"].at[:, s], co(9, X, d, 1)))
    for row, part in ((jnp.where(even, 0, 25), refs["on"]), (jnp.where(even, 25, 0), refs["back"])):
        late.append((part.at[pl.ds(0, 2), s], u0(row, None, d)))
        late.append((part.at[pl.ds(2, 2), s], co(row, None, d, None)))
    return early, late


def target(ref):
    def pick(row, rows, d, lead=None):
        lead = slice(None) if lead is None else lead
        return ref.at[lead, row if rows is None else pl.ds(row, rows), d]

    return pick


def level1_own(refs, u1, src, dst, size, even):
    s, d = pl.ds(src, size), pl.ds(dst, size)
    early = [(refs["u1"].at[:, :, s], u1.at[:, pl.ds(10, X), d])]
    late = []
    for out, part, at_even, at_odd in (
        (early, "nw", 24, 2), (late, "fw", 8, 18), (late, "on1", 0, 26), (late, "back1", 26, 0),
    ):
        row = jnp.where(even, at_even, at_odd)
        out.append((refs[part].at[:, :, s], u1.at[:, pl.ds(row, 2), d]))
    return early, late


def level1_chunk(near_ref, far_ref, u1, src, dst, size, even):
    near, far = jnp.where(even, 18, 4), jnp.where(even, 2, 20)
    s, d = pl.ds(src, size), pl.ds(dst, size)
    return (
        [(near_ref.at[:, :, s], u1.at[:, pl.ds(near, 6), d])],
        [(far_ref.at[:, :, s], u1.at[:, pl.ds(far, 6), d])],
    )


def rim0_kernel(*args):
    refs = dict(zip(NAMES0, args))
    traces_hbm, live_hbm, rim, columns, rows, u0, co, traces, live, sem, sem2 = args[len(NAMES0) :]
    even, gy, shot = place()
    y = by8(jnp.where(gy == 0, Y - G, 0))
    early, late = level0_pieces(refs, target(u0), target(co), y, 0, G, even, shot)
    pieces = early + late
    for part, at in (
        (refs["na"], jnp.where(even, 24, 8)),
        (refs["fa"], jnp.where(even, 8, 24)),
        (refs["on"], jnp.where(even, 0, 32)),
        (refs["back"], jnp.where(even, 32, 0)),
    ):
        for n in range(2):
            pieces.append((part.at[n, pl.ds(Y, G)], rows.at[n, pl.ds(by8(at), X)]))
    copies = run_copies(pieces, sem)
    mask = receivers(traces_hbm, live_hbm, traces, live, sem2)
    for n in range(2):
        rows[n, 16:24] = mask * traces[n + 1]
    wait_all(copies)
    for f in range(2):
        rim[26 * f : 26 * f + 26] = u0[f]
        rim[52 + 26 * f : 78 + 26 * f] = co[f]
    for n in range(2):
        columns[n] = surface_columns(rows[n])
        rim[104 + n] = columns[n, pl.ds(y, G)]


def rim1_kernel(chunk, *args):
    refs = dict(zip(NAMES1, args))
    near, far, out, sem = args[len(NAMES1) :]
    even, gy, shot = place()
    y = by8(jnp.where(gy == 0, Y - G, 0))
    yc = by8(jnp.where(gy == 0, chunk - G, 0))
    pieces = level1_own(refs, out, y, 0, G, even) + level1_chunk(near, far, out, yc, 0, G, even)
    wait_all(run_copies(sum(pieces, []), sem))


def slab_kernel(k, chunks, *args):
    n_in = len(NAMES0) + len(NAMES1)
    refs = dict(zip(NAMES0 + NAMES1, args[:n_in]))
    rest = list(args[n_in:])
    columns = rest.pop(0)
    near_k, far_k = rest.pop(0), rest.pop(0)
    first_slab, last_slab = k == 0, k == len(chunks) - 1
    if first_slab:
        rim0, rim1 = rest.pop(0), rest.pop(0)
    else:
        near_p, far_p, _ = rest.pop(0), rest.pop(0), rest.pop(0)
    out_hbm, u0, u1, u2, u3, co, abc, inj, image, sem, out_sem = rest
    even, gy, shot = place()
    start, width = sum(chunks[:k]), chunks[k]
    lead = G if first_slab else 2 * G
    span = lead + width + (G if last_slab else 0)
    size = span - 2 * G

    def spot(at, length, total):
        return by8(jnp.where(gy == 1, at, total - at - length))

    ahead = 0 if first_slab else 2 * G
    src = spot(start - ahead, ahead + width, Y)
    here = spot(lead - ahead, ahead + width, span)
    dst = by8(here + G)
    batches = [
        level0_pieces(refs, target(u0), target(co), src, dst, ahead + width, even, shot),
        level1_own(refs, u1, src, dst, ahead + width, even),
    ]
    at = by8(spot(lead, width, span) + G)
    batches.append(level1_chunk(near_k, far_k, u1, 0, at, width, even))
    early = [(columns.at[:, pl.ds(src, ahead + width)], inj.at[:, pl.ds(here, ahead + width)])]
    if first_slab:
        at = by8(spot(0, G, span) + G)
        early.append((rim1, u1.at[:, :, pl.ds(at, G)]))
        for f in range(2):
            early.append((rim0.at[pl.ds(26 * f, 26)], u0.at[f, :, pl.ds(at, G)]))
            early.append((rim0.at[pl.ds(52 + 26 * f, 26)], co.at[f, :, pl.ds(at, G)]))
        early.append((rim0.at[pl.ds(104, 2)], inj.at[:, pl.ds(by8(spot(0, G, span)), G)]))
    else:
        before = chunks[k - 1]
        at = by8(spot(0, 2 * G, span) + G)
        at_before = spot(before - 2 * G, 2 * G, before)
        batches.append(level1_chunk(near_p, far_p, u1, at_before, at, 2 * G, even))
    early = sum((a for a, b in batches), early)
    late = sum((b for a, b in batches), [])
    copies = run_copies(early + late, sem)
    if last_slab:
        edge = spot(span - G, G, span)
        for ref in (u0, u1, co):
            for j in range(ref.shape[1]):
                ref[:, j, pl.ds(by8(edge + G), G)] = jnp.zeros((2, G, Z), F32)
        inj[:, pl.ds(edge, G)] = jnp.zeros((2, G, Z), F32)

    lane = lax.broadcasted_iota(jnp.int32, (span, Z), 1)
    first, last = lane == 0, lane == Z - 1
    y = slice(G, G + span)

    def second(row, carry):
        pull, gain, keep = coefficients(co[0, row, y], co[1, row, y])
        abc[0, row, y] = pull
        abc[1, row, y] = gain
        abc[2, row, y] = keep
        for f in range(2):
            centre, total = shifted(u1, f, row + 1, G, span, first, last)
            if f == 1:
                total += jnp.where(first, pltpu.roll(inj[0], 121 - row, 1), 0.0)
            u2[f, row, y] = keep * centre - pull * u0[f, row, y] + gain * total
        return carry

    base = jnp.where(even, 10, 2)
    wait_all(copies[: len(early)])
    lax.fori_loop(0, 14, lambda i, carry: second(base + i, carry), 0, unroll=14)
    wait_all(copies[len(early) :])

    def other_rows(i, carry):
        at_even = jnp.where(i < 10, i, i + 14)
        at_odd = jnp.where(i < 10, i + 16, i - 10)
        return second(jnp.where(even, at_even, at_odd), carry)

    lax.fori_loop(0, 12, other_rows, 0, unroll=12)
    levels = ((u0, 9), (u1, 10), (u2, 9), (u3, 8))
    low = spot((start if first_slab else start - G), size, Y)

    def finish(begin, length, sem_part):
        first_, last_ = first[:length], last[:length]
        lo = 2 * G + begin
        yy = slice(lo, lo + length)

        def third(row, carry):
            for f in range(2):
                centre, total = shifted(u2, f, row + 1, lo, length, first_, last_)
                if f == 1:
                    column = inj[1, G + begin : G + begin + length]
                    total += jnp.where(first_, pltpu.roll(column, 120 - row, 1), 0.0)
                u3[f, row, yy] = (
                    abc[2, row + 1, yy] * centre
                    - abc[0, row + 1, yy] * u1[f, row + 2, yy]
                    + abc[1, row + 1, yy] * total
                )
            return carry

        lax.fori_loop(0, 24, third, 0, unroll=24)

        def products(g, carry):
            cells = pl.ds(by8(lo + g * G), G)
            to = pl.ds(by8(begin + g * G), G)
            for parity in range(2):
                for tile in range(3):
                    rows_a = [-8 + parity + 8 * tile + 2 * j for j in range(4)]
                    held = [[ref[0, a + o, cells] for ref, o in levels] for a in rows_a]
                    for b in range(-8 + parity, 16, 2):
                        wanted = [
                            j for j, a in enumerate(rows_a) if 0 <= a + b < 16 and abs(b - a) <= 16
                        ]
                        if not wanted:
                            continue
                        right = [ref[1, b + o, cells] for ref, o in levels]
                        for j in wanted:
                            a = rows_a[j]
                            p = [l * r for l, r in zip(held[j], right)]
                            image[(b - a) // 2 + 8, (a + b) // 2, to] = (p[0] + p[1]) + (
                                p[2] + p[3]
                            )
            return carry

        lax.fori_loop(0, length // G, products, 0)
        copy = pltpu.make_async_copy(
            image.at[:, :, pl.ds(begin, length)],
            out_hbm.at[:, :, pl.ds(by8(low + begin), length)],
            sem_part,
        )
        copy.start()
        return copy

    groups = size // G
    cuts = [groups * j // PARTS * G for j in range(PARTS + 1)]
    wait_all(
        [finish(a, b - a, out_sem.at[j]) for j, (a, b) in enumerate(zip(cuts, cuts[1:]))]
    )


def call(kernel, outs, args, specs, scratch, name, out_specs=None, **extra):
    return pl.pallas_call(
        kernel,
        out_shape=[jax.ShapeDtypeStruct(s, F32) for s in outs],
        in_specs=specs,
        out_specs=out_specs or [HBM] * len(outs),
        scratch_shapes=scratch,
        compiler_params=pltpu.CompilerParams(vmem_limit_bytes=48 << 20),
        name=name,
        **extra,
    )(*args)


def after(value, *earlier):
    return lax.optimization_barrier((value, *earlier))[0]


def shards(fields_now, fields_later, velocity_term, damping, traces, receiver_live):
    count = lax.axis_size("gx")
    swap_x = [(i, i ^ 1) for i in range(count)]
    onward = [(i, i + 2) for i in range(0, count - 2, 2)]
    onward += [(i, i - 2) for i in range(3, count, 2)]
    backward = [(b, a) for a, b in onward]
    swap = [(0, 1), (1, 0)]
    dma = pltpu.SemaphoreType.DMA
    vm = pltpu.VMEM
    u0 = fields_now
    small = [vm((STEPS - 1, X, Y), F32), vm((X, Y), jnp.int32)]
    params = (u0, fields_later, velocity_term, damping, traces, receiver_live)
    u0, fields_later, velocity_term, damping, traces, receiver_live = (
        pltpu.with_memory_space_constraint(a, pltpu.HBM) for a in params
    )

    edge, brink = call(
        edge_kernel, [(2, 2, Y, Z), (2, X, G, Z)], (u0,), [HBM], [dma((3,))], "edge"
    )
    mine, rest, on0, back0 = call(
        prep_kernel,
        [(X, Y + G, Z), (2, 6, Y, Z), (4, Y + G, Z), (4, Y + G, Z)],
        (u0, velocity_term, damping, after(traces, brink), receiver_live),
        [HBM] * 5,
        [vm((2, X, Y), F32), *small, dma((8,)), dma((8,))],
        "prep",
    )
    near_edge = lax.ppermute(edge, "gx", swap_x)
    from_on0 = lax.ppermute(after(on0, near_edge), "gx", onward)
    beside = lax.ppermute(brink, "gy", swap)
    near_mine = lax.ppermute(mine, "gx", swap_x)
    far_edge = lax.ppermute(after(near_edge, beside), "gx", onward)
    near_rest = lax.ppermute(after(rest, near_edge, far_edge), "gx", swap_x)
    from_back0 = lax.ppermute(after(back0, near_rest), "gx", backward)

    u1, on1, brow, *parts = call(
        functools.partial(first_kernel, CHUNKS),
        [(2, X, Y, Z), (2, 2, Y, Z), (2, 2, Y, Z)] + [(2, 6, w, Z) for w in CHUNKS],
        (u0, fields_later, velocity_term, damping, near_edge, far_edge, beside, traces,
         receiver_live),
        [HBM] * 9,
        [
            vm((2, X + 2, Y + 2 * G, Z), F32),
            vm((2, X, Y, Z), F32),
            vm((X, Y, Z), F32),
            vm((X, Y, Z), F32),
            vm((2, X, Y, Z), F32),
            *small,
            dma((10 + len(CHUNKS),)),
            dma((2,)),
        ],
        "first",
    )
    far_mine = lax.ppermute(after(near_mine, u1, from_on0), "gx", onward)
    near_other = lax.ppermute(after(near_mine, u1, from_on0), "shot", swap)
    from_back1 = lax.ppermute(brow, "gx", backward)
    near_brow = lax.ppermute(after(brow, beside, near_mine), "gx", swap_x)
    near0 = lax.ppermute(after(parts[0], near_rest), "gx", swap_x)
    far_rest = lax.ppermute(after(near_rest, far_mine, from_back1), "gx", onward)
    from_on1 = lax.ppermute(after(on1, near_rest), "gx", onward)
    far_brow = lax.ppermute(after(from_back1, near_brow), "gx", swap_x)
    far_other = lax.ppermute(far_mine, "shot", swap)
    near1 = lax.ppermute(after(parts[1], near_other), "gx", swap_x)
    far0 = lax.ppermute(near0, "gx", onward)
    far1 = lax.ppermute(after(near1, from_on1, far_other), "gx", onward)
    near_chunks, far_chunks = [near0, near1], [far0, far1]

    base0 = (
        near_edge, near_rest, near_mine, near_other,
        far_edge, far_rest, far_mine, far_other,
        u0, velocity_term, damping, from_on0, from_back0,
    )
    base1 = (u1, from_on1, from_back1, near_brow, far_brow)
    rim0, columns = call(
        rim0_kernel,
        [(106, G, Z), (2, Y, Z)],
        (*base0, traces, receiver_live),
        [HBM] * (len(base0) + 2),
        [
            vm((2, 40, Y), F32),
            vm((2, 26, G, Z), F32),
            vm((2, 26, G, Z), F32),
            *small,
            dma((25,)),
            dma((2,)),
        ],
        "rim0",
        [VMEM, VMEM],
    )
    rim0 = lax.ppermute(rim0, "gy", swap)
    (rim1,) = call(
        functools.partial(rim1_kernel, CHUNKS[0]),
        [(2, 28, G, Z)],
        (*base1, near_chunks[0], far_chunks[0]),
        [HBM] * 7,
        [dma((7,))],
        "rim1",
        [VMEM],
    )
    rim1 = lax.ppermute(rim1, "gy", swap)

    image = None
    for k, width in enumerate(CHUNKS):
        first_slab, last_slab = k == 0, k == len(CHUNKS) - 1
        span = (G if first_slab else 2 * G) + width + (G if last_slab else 0)
        args = [*base0, *base1, columns, near_chunks[k], far_chunks[k]]
        if first_slab:
            args += [rim0, rim1]
        else:
            args += [near_chunks[k - 1], far_chunks[k - 1], image]
        wide = span + 2 * G
        (image,) = call(
            functools.partial(slab_kernel, k, CHUNKS),
            [(2 * LAG_HALF + 1, X, Y, Z)],
            args,
            [HBM] * len(args),
            [
                vm((2, 26, wide, Z), F32),
                vm((2, 28, wide, Z), F32),
                vm((2, 26, wide, Z), F32),
                vm((2, 24, wide, Z), F32),
                vm((2, 26, wide, Z), F32),
                vm((3, 26, wide, Z), F32),
                vm((2, span, Z), F32),
                vm((2 * LAG_HALF + 1, X, span - 2 * G, Z), F32),
                dma((32,)),
                dma((max(1, (span - 2 * G) // G),)),
            ],
            f"slab{k}",
            input_output_aliases={} if first_slab else {len(args) - 1: 0},
        )
    return image


def solution(mesh):
    placed = (
        P("shot", "gx", "gy", None),
        P("shot", "gx", "gy", None),
        P("gx", "gy", None),
        P("gx", "gy", None),
        P("shot", "gx", "gy"),
        P("gx", "gy"),
    )

    def body(fields_now, *others):
        fits = fields_now.shape == (2, X, 128, 128) and mesh.shape["gx"] % 2 == 0
        fits = fits and mesh.shape["gy"] == 2 and mesh.shape["shot"] == 2
        return (shards if fits else plain)(fields_now, *others)

    return jax.shard_map(
        body, mesh=mesh, in_specs=placed, out_specs=P("shot", "gx", "gy", None), check_vma=False
    )
```

time: 117 us -> 89.2 us (0.76)
  waiting for transfers between devices: 45.9 us -> 29.2 us
  local copies, waits for them, and re-layouts: 9.07 us -> 0.01 us
    ppermute x1, waiting for transfers between devices: 17.9 us -> 5.4 us  [shards(): near_edge = lax.ppermute(edge, 'gx', swap_x)]
    ppermute x14 -> x15, waiting for transfers between devices: 11.2 us -> 22.3 us  [the longest x1 6.97 us: shards(): from_back1 = lax.ppermute(brow, 'gx', backward)]
    ppermute x1, waiting for transfers between devices: 10.7 us -> 0.01 us  [shards(): near_mine = lax.ppermute(mine, 'gx', swap_x)]
    unnamed x30 -> x6, local copies, waits for them, and re-layouts: 9.07 us -> 0.01 us
    ppermute x1, waiting for transfers between devices: 4.56 us -> 0.01 us  [shards(): far_other = lax.ppermute(far_mine, 'shot', swap)]
    ppermute x1, starting transfers between devices: 3 us -> 0.17 us  [shards(): near_mine = lax.ppermute(mine, 'gx', swap_x)]
    ppermute x14 -> x15, starting transfers between devices: 32.1 us -> 33.4 us  [the longest x1 4.05 us: shards(): far_edge = lax.ppermute(after(near_edge, beside), 'gx', onward)]
  transfers between devices with their start and end apart: 20 -> 21, of which waited for: 6 -> 9; matrix products, arithmetic and copies ran while one was open for 0% -> 0% of each run, Pallas kernels for 14% -> 14%
where the time goes in v2:
time: 89.2 us; the launch traced here: 88.7 us
  starting transfers between devices  37.6 us (42%)
  waiting for transfers between devices  29.2 us (33%)
  Pallas kernels  21.7 us (24%)
    pallas_call x7, Pallas kernels, call(): pl.pallas_call(kernel, out_shape=[jax.ShapeDtypeStruct(s, F32) for s in o...  21.7 us
    ppermute x1, waiting for transfers between devices, shards(): from_back1 = lax.ppermute(brow, 'gx', backward)  6.97 us
    ppermute x1, waiting for transfers between devices, shards(): near_brow = lax.ppermute(after(brow, beside, near_mine), 'gx', swap_x)  5.92 us
    ppermute x1, waiting for transfers between devices, shards(): near_edge = lax.ppermute(edge, 'gx', swap_x)  5.4 us
    ppermute x1, starting transfers between devices, shards(): far_edge = lax.ppermute(after(near_edge, beside), 'gx', onward)  4.05 us
    ppermute x1, waiting for transfers between devices, shards(): near0 = lax.ppermute(after(parts[0], near_rest), 'gx', swap_x)  3.76 us
    ppermute x1, starting transfers between devices, shards(): far_mine = lax.ppermute(after(near_mine, u1, from_on0), 'gx', onward)  3.52 us
    ppermute x1, starting transfers between devices, shards(): lax.ppermute(after(near_rest, far_mine, from_back1), 'gx', onward)  3.5 us
  transfers between devices with their start and end apart: 21, of which 9 were waited for; matrix products, arithmetic and copies ran while one was open for 0% of the time, Pallas kernels for 14%

profile of v2, /device:TPU:0, one launch (start us, length us, event | category | flops | bytes accessed | tf_op | source)
XLA Modules:
  0.0 88.7 jit_solution(3700660768282724807)
XLA Ops:
  0.0 1.0 %edge.1 = (f32[2,2,128,128]{3,2,1,0:T(8,128)S(1)}, f32[2,8,8,128]{3,2,1,0:T(8,128)S(1)}) custom-call(f32[2,8,128,128]{3,2,1,0:T(8,128)} %args_8_.7), custom_call_target="tpu_custom_call" | custom-call | tf_op jit(solution)/shard_map/edge/pallas_call | solution.py:462
  1.0 3.0 %collective-permute-start = (f32[2,2,128,128]{3,2,1,0:T(8,128)S(1)}, f32[2,2,128,128]{3,2,1,0:T(8,128)S(1)}, u32[]{:S(2)}, u32[]{:S(2)}) collective-permute-start(f32[2,2,128,128]{3,2,1,0:T(8,128)S(1)} %get-tuple-element.31), channel_id=1, source_target_pairs={{0,2},{2,0},{4,6},{6,4},{8,10},{10,8},{12,14},{14,12},{1,3},{3,1},... | collective-permute-start | bytes 786440 | tf_op jit(solution)/shard_map/ppermute | solution.py:505
  4.0 0.0 collective-permute-start.1
  4.0 1.5 %prep.1 = (f32[8,136,128]{2,1,0:T(8,128)S(1)}, f32[2,6,128,128]{3,2,1,0:T(8,128)S(1)}, f32[4,136,128]{2,1,0:T(8,128)S(1)}, f32[4,136,128]{2,1,0:T(8,128)S(1)}) custom-call(f32[2,8,128,128]{3,2,1,0:T(8,128)} %args_8_.7, f32[8,128,128]{2,1,0:T(8,128)} %args_9_.5, f32[8,128,128]{2,1,0:T(8,128)} %args_10_.5, f32[3,8,128]{2,1,0:T(8,128)} %args_13_.1, ...), custom_call_target="tpu_custom_call" | custom-call | tf_op jit(solution)/shard_map/prep/pallas_call | solution.py:462
  5.6 0.2 collective-permute-start.4
  5.7 0.0 collective-permute-done.1.args_6_
  5.7 5.4 %collective-permute-done.args_4_.args_0_ = f32[2,2,128,128]{3,2,1,0:T(8,128)S(1)} collective-permute-done((f32[2,2,128,128]{3,2,1,0:T(8,128)S(1)}, f32[2,2,128,128]{3,2,1,0:T(8,128)S(1)}, u32[]{:S(2)}, u32[]{:S(2)}) %collective-permute-start) | collective-permute-done | bytes 262176 | tf_op jit(solution)/shard_map/ppermute | solution.py:505
  11.1 4.1 %collective-permute-start.2 = (f32[2,2,128,128]{3,2,1,0:T(8,128)S(1)}, f32[2,2,128,128]{3,2,1,0:T(8,128)S(1)}, u32[]{:S(2)}, u32[]{:S(2)}) collective-permute-start(f32[2,2,128,128]{3,2,1,0:T(8,128)S(1)} %collective-permute-done.args_4_.args_0_), channel_id=1, source_target_pairs={{0,4},{4,8},{8,12},{6,2},{10,6},{14,10},{1,5},{5,9},{9,13},{7,3},{... | collective-permute-start | bytes 786440 | tf_op jit(solution)/shard_map/ppermute | solution.py:509
  15.2 3.5 %collective-permute-start.5 = (f32[4,136,128]{2,1,0:T(8,128)S(1)}, f32[4,136,128]{2,1,0:T(8,128)S(1)}, u32[]{:S(2)}, u32[]{:S(2)}) collective-permute-start(f32[4,136,128]{2,1,0:T(8,128)S(1)} %get-tuple-element.40), channel_id=1, source_target_pairs={{0,4},{4,8},{8,12},{6,2},{10,6},{14,10},{1,5},{5,9},{9,13},{7,3},{... | collective-permute-start | bytes 835592 | tf_op jit(solution)/shard_map/ppermute | solution.py:506
  18.7 3.1 %collective-permute-done.2.args_5_.args_4_ = f32[2,2,128,128]{3,2,1,0:T(8,128)S(1)} collective-permute-done((f32[2,2,128,128]{3,2,1,0:T(8,128)S(1)}, f32[2,2,128,128]{3,2,1,0:T(8,128)S(1)}, u32[]{:S(2)}, u32[]{:S(2)}) %collective-permute-start.2) | collective-permute-done | bytes 262176 | tf_op jit(solution)/shard_map/ppermute | solution.py:509
  21.8 2.3 %collective-permute-start.3 = (f32[2,6,128,128]{3,2,1,0:T(8,128)S(1)}, f32[2,6,128,128]{3,2,1,0:T(8,128)S(1)}, u32[]{:S(2)}, u32[]{:S(2)}) collective-permute-start(f32[2,6,128,128]{3,2,1,0:T(8,128)S(1)} %get-tuple-element.36), channel_id=1, source_target_pairs={{0,2},{2,0},{4,6},{6,4},{8,10},{10,8},{12,14},{14,12},{1,3},{3,1},... | collective-permute-start | bytes 2359304 | tf_op jit(solution)/shard_map/ppermute | solution.py:510
  24.1 3.0 %first.1 = (f32[2,8,128,128]{3,2,1,0:T(8,128)S(1)}, f32[2,2,128,128]{3,2,1,0:T(8,128)S(1)}, f32[2,2,128,128]{3,2,1,0:T(8,128)S(1)}, f32[2,6,64,128]{3,2,1,0:T(8,128)S(1)}, f32[2,6,64,128]{3,2,1,0:T(8,128)S(1)}) custom-call(f32[2,8,128,128]{3,2,1,0:T(8,128)} %args_8_.7, f32[2,8,128,128]{3,2,1,0:T(8,128)} %args_1_.4, f32[8,128,128]{2,1,0:T(8,128)} %args_9_.5, ...), custom_call_target="tpu_custom_call" | custom-call | tf_op jit(solution)/shard_map/first/pallas_call | solution.py:462
  27.1 0.0 collective-permute-done.5.args_11_
  27.1 0.0 collective-permute-done.4.args_2_
  27.1 3.5 %collective-permute-start.7 = (f32[8,136,128]{2,1,0:T(8,128)S(1)}, f32[8,136,128]{2,1,0:T(8,128)S(1)}, u32[]{:S(2)}, u32[]{:S(2)}) collective-permute-start(f32[8,136,128]{2,1,0:T(8,128)S(1)} %collective-permute-done.4.args_2_), channel_id=1, source_target_pairs={{0,4},{4,8},{8,12},{6,2},{10,6},{14,10},{1,5},{5,9},{9,13},{7,3},{... | collective-permute-start | bytes 1671176 | tf_op jit(solution)/shard_map/ppermute | solution.py:531
  30.7 1.6 %collective-permute-start.6 = (f32[8,136,128]{2,1,0:T(8,128)S(1)}, f32[8,136,128]{2,1,0:T(8,128)S(1)}, u32[]{:S(2)}, u32[]{:S(2)}) collective-permute-start(f32[8,136,128]{2,1,0:T(8,128)S(1)} %collective-permute-done.4.args_2_), channel_id=1, source_target_pairs={{0,16},{16,0},{1,17},{17,1},{2,18},{18,2},{3,19},{19,3},{4,20},{20... | collective-permute-start | bytes 1671176 | tf_op jit(solution)/shard_map/ppermute | solution.py:532
  32.2 1.3 %collective-permute-start.8 = (f32[2,2,128,128]{3,2,1,0:T(8,128)S(1)}, f32[2,2,128,128]{3,2,1,0:T(8,128)S(1)}, u32[]{:S(2)}, u32[]{:S(2)}) collective-permute-start(f32[2,2,128,128]{3,2,1,0:T(8,128)S(1)} %get-tuple-element.48), channel_id=1, source_target_pairs={{4,0},{8,4},{12,8},{2,6},{6,10},{10,14},{5,1},{9,5},{13,9},{3,7},{... | collective-permute-start | bytes 786440 | tf_op jit(solution)/shard_map/ppermute | solution.py:533
  33.5 7.0 %collective-permute-done.8.args_2_.args_15_ = f32[2,2,128,128]{3,2,1,0:T(8,128)S(1)} collective-permute-done((f32[2,2,128,128]{3,2,1,0:T(8,128)S(1)}, f32[2,2,128,128]{3,2,1,0:T(8,128)S(1)}, u32[]{:S(2)}, u32[]{:S(2)}) %collective-permute-start.8) | collective-permute-done | bytes 262176 | tf_op jit(solution)/shard_map/ppermute | solution.py:533
  40.5 0.0 collective-permute-done.7.args_6_
  40.5 0.0 collective-permute-done.3.args_1_
  40.5 3.5 %collective-permute-start.9 = (f32[2,6,128,128]{3,2,1,0:T(8,128)S(1)}, f32[2,6,128,128]{3,2,1,0:T(8,128)S(1)}, u32[]{:S(2)}, u32[]{:S(2)}) collective-permute-start(f32[2,6,128,128]{3,2,1,0:T(8,128)S(1)} %collective-permute-done.3.args_1_), channel_id=1, source_target_pairs={{0,4},{4,8},{8,12},{6,2},{10,6},{14,10},{1,5},{5,9},{9,13},{7,3},{... | collective-permute-start | bytes 2359304 | tf_op jit(solution)/shard_map/ppermute | solution.py:536
  44.0 0.8 collective-permute-start.10
  44.8 0.0 collective-permute-start.13
  44.8 2.0 %collective-permute-start.17 = (f32[2,6,64,128]{3,2,1,0:T(8,128)S(1)}, f32[2,6,64,128]{3,2,1,0:T(8,128)S(1)}, u32[]{:S(2)}, u32[]{:S(2)}) collective-permute-start(f32[2,6,64,128]{3,2,1,0:T(8,128)S(1)} %get-tuple-element.55), channel_id=1, source_target_pairs={{0,2},{2,0},{4,6},{6,4},{8,10},{10,8},{12,14},{14,12},{1,3},{3,1},... | collective-permute-start | bytes 1179656 | tf_op jit(solution)/shard_map/ppermute | solution.py:535
  46.9 0.0 collective-permute-done.6.args_3_
  46.9 1.3 %collective-permute-start.11 = (f32[4,136,128]{2,1,0:T(8,128)S(1)}, f32[4,136,128]{2,1,0:T(8,128)S(1)}, u32[]{:S(2)}, u32[]{:S(2)}) collective-permute-start(f32[4,136,128]{2,1,0:T(8,128)S(1)} %get-tuple-element.45), channel_id=1, source_target_pairs={{4,0},{8,4},{12,8},{2,6},{6,10},{10,14},{5,1},{9,5},{13,9},{3,7},{... | collective-permute-start | bytes 835592 | tf_op jit(solution)/shard_map/ppermute | solution.py:511
  48.1 5.9 %collective-permute-done.13.args_3_.args_16_ = f32[2,2,128,128]{3,2,1,0:T(8,128)S(1)} collective-permute-done((f32[2,2,128,128]{3,2,1,0:T(8,128)S(1)}, f32[2,2,128,128]{3,2,1,0:T(8,128)S(1)}, u32[]{:S(2)}, u32[]{:S(2)}) %collective-permute-start.13) | collective-permute-done | bytes 262176 | tf_op jit(solution)/shard_map/ppermute | solution.py:534
  54.1 0.0 collective-permute-start.15
  54.1 1.2 %collective-permute-done.11.args_12_ = f32[4,136,128]{2,1,0:T(8,128)S(1)} collective-permute-done((f32[4,136,128]{2,1,0:T(8,128)S(1)}, f32[4,136,128]{2,1,0:T(8,128)S(1)}, u32[]{:S(2)}, u32[]{:S(2)}) %collective-permute-start.11) | collective-permute-done | bytes 278560 | tf_op jit(solution)/shard_map/ppermute | solution.py:511
  55.3 3.4 %collective-permute-start.12 = (f32[2,2,128,128]{3,2,1,0:T(8,128)S(1)}, f32[2,2,128,128]{3,2,1,0:T(8,128)S(1)}, u32[]{:S(2)}, u32[]{:S(2)}) collective-permute-start(f32[2,2,128,128]{3,2,1,0:T(8,128)S(1)} %get-tuple-element.47), channel_id=1, source_target_pairs={{0,4},{4,8},{8,12},{6,2},{10,6},{14,10},{1,5},{5,9},{9,13},{7,3},{... | collective-permute-start | bytes 786440 | tf_op jit(solution)/shard_map/ppermute | solution.py:537
  58.7 3.8 %collective-permute-done.17.args_5_.args_19_.args_21_ = f32[2,6,64,128]{3,2,1,0:T(8,128)S(1)} collective-permute-done((f32[2,6,64,128]{3,2,1,0:T(8,128)S(1)}, f32[2,6,64,128]{3,2,1,0:T(8,128)S(1)}, u32[]{:S(2)}, u32[]{:S(2)}) %collective-permute-start.17) | collective-permute-done | bytes 393248 | tf_op jit(solution)/shard_map/ppermute | solution.py:535
  62.5 3.4 %collective-permute-start.18 = (f32[2,6,64,128]{3,2,1,0:T(8,128)S(1)}, f32[2,6,64,128]{3,2,1,0:T(8,128)S(1)}, u32[]{:S(2)}, u32[]{:S(2)}) collective-permute-start(f32[2,6,64,128]{3,2,1,0:T(8,128)S(1)} %collective-permute-done.17.args_5_.args_19_.args_21_), channel_id=1, source_target_pairs={{0,4},{4,8},{8,12},{6,2},{10,6},{14,10},{1,5},{5,9},{9,13},{7,3},{... | collective-permute-start | bytes 1179656 | tf_op jit(solution)/shard_map/ppermute | solution.py:541
  66.0 0.0 collective-permute-done.10.args_7_
  66.0 0.1 collective-permute-start.14
  66.0 0.0 collective-permute-done.9.args_5_
  66.1 1.5 %rim0.1 = (f32[106,8,128]{2,1,0:T(8,128)S(1)}, f32[2,128,128]{2,1,0:T(8,128)S(1)}) custom-call(f32[2,2,128,128]{3,2,1,0:T(8,128)S(1)} %collective-permute-done.args_4_.args_0_, f32[2,6,128,128]{3,2,1,0:T(8,128)S(1)} %collective-permute-done.3.args_1_, f32[8,136,128]{2,1,0:T(8,128)S(1)} %collective-permute-done.4.args_2_, ...), custom_call_target="tpu_custom_call" | custom-call | tf_op jit(solution)/shard_map/rim0/pallas_call | solution.py:462
  67.5 0.1 collective-permute-start.19
  67.6 0.4 collective-permute-done.15.args_19_
  68.0 0.0 collective-permute-done.12.args_1_.args_14_
  68.1 3.4 %collective-permute-start.16 = (f32[2,6,64,128]{3,2,1,0:T(8,128)S(1)}, f32[2,6,64,128]{3,2,1,0:T(8,128)S(1)}, u32[]{:S(2)}, u32[]{:S(2)}) collective-permute-start(f32[2,6,64,128]{3,2,1,0:T(8,128)S(1)} %collective-permute-done.15.args_19_), channel_id=1, source_target_pairs={{0,4},{4,8},{8,12},{6,2},{10,6},{14,10},{1,5},{5,9},{9,13},{7,3},{... | collective-permute-start | bytes 1179656 | tf_op jit(solution)/shard_map/ppermute | solution.py:542
  71.5 0.9 %collective-permute-done.14.args_4_.args_17_ = f32[2,2,128,128]{3,2,1,0:T(8,128)S(1)} collective-permute-done((f32[2,2,128,128]{3,2,1,0:T(8,128)S(1)}, f32[2,2,128,128]{3,2,1,0:T(8,128)S(1)}, u32[]{:S(2)}, u32[]{:S(2)}) %collective-permute-start.14) | collective-permute-done | bytes 262176 | tf_op jit(solution)/shard_map/ppermute | solution.py:538
  72.4 0.0 collective-permute-done.18.args_6_.args_20_.args_22_
  72.4 0.1 rim1.1
  72.5 0.1 collective-permute-start.20
  72.6 1.5 %collective-permute-done.20.args_22_ = f32[2,28,8,128]{3,2,1,0:T(8,128)S(1)} collective-permute-done((f32[2,28,8,128]{3,2,1,0:T(8,128)S(1)}, f32[2,28,8,128]{3,2,1,0:T(8,128)S(1)}, u32[]{:S(2)}, u32[]{:S(2)}) %collective-permute-start.20) | collective-permute-done | bytes 229408 | tf_op jit(solution)/shard_map/ppermute | solution.py:577
  74.1 0.0 collective-permute-done.19.args_21_
  74.1 6.6 %slab0.1.args_23_ = f32[17,8,128,128]{3,2,1,0:T(8,128)} custom-call(f32[2,2,128,128]{3,2,1,0:T(8,128)S(1)} %collective-permute-done.args_4_.args_0_, f32[2,6,128,128]{3,2,1,0:T(8,128)} %copy-done.1, f32[8,136,128]{2,1,0:T(8,128)S(1)} %collective-permute-done.4.args_2_, f32[8,136,128]{2,1,0:T(8,128)S(1)} %collective-permute-done.6.args_3_, ...), custom_call_target="tpu_custom_call" | custom-call | tf_op jit(solution)/shard_map/slab0/pallas_call | solution.py:462
  80.7 8.0 %slab1.1 = f32[17,8,128,128]{3,2,1,0:T(8,128)} custom-call(f32[2,2,128,128]{3,2,1,0:T(8,128)S(1)} %collective-permute-done.args_4_.args_0_, f32[2,6,128,128]{3,2,1,0:T(8,128)} %copy-done.1, f32[8,136,128]{2,1,0:T(8,128)S(1)} %collective-permute-done.4.args_2_, f32[8,136,128]{2,1,0:T(8,128)S(1)} %collective-permute-done.6.args_3_, ...), custom_call_target="tpu_custom_call", output_to_operand_aliasing={{}: (23, {})} | custom-call | tf_op jit(solution)/shard_map/slab1/pallas_call | solution.py:462
  (7 shorter events, 0.0 us)
Async XLA Ops:
  1.0 10.1 %collective-permute-start = (f32[2,2,128,128]{3,2,1,0:T(8,128)S(1)}, f32[2,2,128,128]{3,2,1,0:T(8,128)S(1)}, u32[]{:S(2)}, u32[]{:S(2)}) collective-permute-start(f32[2,2,128,128]{3,2,1,0:T(8,128)S(1)} %get-tuple-element.31), channel_id=1, source_target_pairs={{0,2},{2,0},{4,6},{6,4},{8,10},{10,8},{12,14},{14,12},{1,3},{3,1},... | collective-permute-start | bytes 786440 | tf_op jit(solution)/shard_map/ppermute | solution.py:505
  4.0 1.7 %collective-permute-start.1 = (f32[2,8,8,128]{3,2,1,0:T(8,128)S(1)}, f32[2,8,8,128]{3,2,1,0:T(8,128)S(1)}, u32[]{:S(2)}, u32[]{:S(2)}) collective-permute-start(f32[2,8,8,128]{3,2,1,0:T(8,128)S(1)} %get-tuple-element.32), channel_id=1, source_target_pairs={{0,1},{1,0},{2,3},{3,2},{4,5},{5,4},{6,7},{7,6},{8,9},{9,8},{10,11... | collective-permute-start | bytes 196616 | tf_op jit(solution)/shard_map/ppermute | solution.py:507
  5.6 21.6 %collective-permute-start.4 = (f32[8,136,128]{2,1,0:T(8,128)S(1)}, f32[8,136,128]{2,1,0:T(8,128)S(1)}, u32[]{:S(2)}, u32[]{:S(2)}) collective-permute-start(f32[8,136,128]{2,1,0:T(8,128)S(1)} %get-tuple-element.37), channel_id=1, source_target_pairs={{0,2},{2,0},{4,6},{6,4},{8,10},{10,8},{12,14},{14,12},{1,3},{3,1},... | collective-permute-start | bytes 1671176 | tf_op jit(solution)/shard_map/ppermute | solution.py:508
  11.1 10.7 %collective-permute-start.2 = (f32[2,2,128,128]{3,2,1,0:T(8,128)S(1)}, f32[2,2,128,128]{3,2,1,0:T(8,128)S(1)}, u32[]{:S(2)}, u32[]{:S(2)}) collective-permute-start(f32[2,2,128,128]{3,2,1,0:T(8,128)S(1)} %collective-permute-done.args_4_.args_0_), channel_id=1, source_target_pairs={{0,4},{4,8},{8,12},{6,2},{10,6},{14,10},{1,5},{5,9},{9,13},{7,3},{... | collective-permute-start | bytes 786440 | tf_op jit(solution)/shard_map/ppermute | solution.py:509
  15.2 11.9 %collective-permute-start.5 = (f32[4,136,128]{2,1,0:T(8,128)S(1)}, f32[4,136,128]{2,1,0:T(8,128)S(1)}, u32[]{:S(2)}, u32[]{:S(2)}) collective-permute-start(f32[4,136,128]{2,1,0:T(8,128)S(1)} %get-tuple-element.40), channel_id=1, source_target_pairs={{0,4},{4,8},{8,12},{6,2},{10,6},{14,10},{1,5},{5,9},{9,13},{7,3},{... | collective-permute-start | bytes 835592 | tf_op jit(solution)/shard_map/ppermute | solution.py:506
  21.8 18.7 %collective-permute-start.3 = (f32[2,6,128,128]{3,2,1,0:T(8,128)S(1)}, f32[2,6,128,128]{3,2,1,0:T(8,128)S(1)}, u32[]{:S(2)}, u32[]{:S(2)}) collective-permute-start(f32[2,6,128,128]{3,2,1,0:T(8,128)S(1)} %get-tuple-element.36), channel_id=1, source_target_pairs={{0,2},{2,0},{4,6},{6,4},{8,10},{10,8},{12,14},{14,12},{1,3},{3,1},... | collective-permute-start | bytes 2359304 | tf_op jit(solution)/shard_map/ppermute | solution.py:510
  27.1 47.0 %copy-start = (f32[2,8,128,128]{3,2,1,0:T(8,128)}, f32[2,8,128,128]{3,2,1,0:T(8,128)S(1)}, u32[]{:S(2)}) copy-start(f32[2,8,128,128]{3,2,1,0:T(8,128)S(1)} %get-tuple-element.38.args_0_.args_13_) | copy-start | bytes 3145732
  27.1 13.4 %collective-permute-start.7 = (f32[8,136,128]{2,1,0:T(8,128)S(1)}, f32[8,136,128]{2,1,0:T(8,128)S(1)}, u32[]{:S(2)}, u32[]{:S(2)}) collective-permute-start(f32[8,136,128]{2,1,0:T(8,128)S(1)} %collective-permute-done.4.args_2_), channel_id=1, source_target_pairs={{0,4},{4,8},{8,12},{6,2},{10,6},{14,10},{1,5},{5,9},{9,13},{7,3},{... | collective-permute-start | bytes 1671176 | tf_op jit(solution)/shard_map/ppermute | solution.py:531
  30.7 16.2 %collective-permute-start.6 = (f32[8,136,128]{2,1,0:T(8,128)S(1)}, f32[8,136,128]{2,1,0:T(8,128)S(1)}, u32[]{:S(2)}, u32[]{:S(2)}) collective-permute-start(f32[8,136,128]{2,1,0:T(8,128)S(1)} %collective-permute-done.4.args_2_), channel_id=1, source_target_pairs={{0,16},{16,0},{1,17},{17,1},{2,18},{18,2},{3,19},{19,3},{4,20},{20... | collective-permute-start | bytes 1671176 | tf_op jit(solution)/shard_map/ppermute | solution.py:532
  32.2 8.3 %collective-permute-start.8 = (f32[2,2,128,128]{3,2,1,0:T(8,128)S(1)}, f32[2,2,128,128]{3,2,1,0:T(8,128)S(1)}, u32[]{:S(2)}, u32[]{:S(2)}) collective-permute-start(f32[2,2,128,128]{3,2,1,0:T(8,128)S(1)} %get-tuple-element.48), channel_id=1, source_target_pairs={{4,0},{8,4},{12,8},{2,6},{6,10},{10,14},{5,1},{9,5},{13,9},{3,7},{... | collective-permute-start | bytes 786440 | tf_op jit(solution)/shard_map/ppermute | solution.py:533
  40.5 33.6 %copy-start.1 = (f32[2,6,128,128]{3,2,1,0:T(8,128)}, f32[2,6,128,128]{3,2,1,0:T(8,128)S(1)}, u32[]{:S(2)}) copy-start(f32[2,6,128,128]{3,2,1,0:T(8,128)S(1)} %collective-permute-done.3.args_1_) | copy-start | bytes 2359300
  40.5 25.5 %collective-permute-start.9 = (f32[2,6,128,128]{3,2,1,0:T(8,128)S(1)}, f32[2,6,128,128]{3,2,1,0:T(8,128)S(1)}, u32[]{:S(2)}, u32[]{:S(2)}) collective-permute-start(f32[2,6,128,128]{3,2,1,0:T(8,128)S(1)} %collective-permute-done.3.args_1_), channel_id=1, source_target_pairs={{0,4},{4,8},{8,12},{6,2},{10,6},{14,10},{1,5},{5,9},{9,13},{7,3},{... | collective-permute-start | bytes 2359304 | tf_op jit(solution)/shard_map/ppermute | solution.py:536
  44.0 21.9 %collective-permute-start.10 = (f32[8,136,128]{2,1,0:T(8,128)S(1)}, f32[8,136,128]{2,1,0:T(8,128)S(1)}, u32[]{:S(2)}, u32[]{:S(2)}) collective-permute-start(f32[8,136,128]{2,1,0:T(8,128)S(1)} %collective-permute-done.7.args_6_), channel_id=1, source_target_pairs={{0,16},{16,0},{1,17},{17,1},{2,18},{18,2},{3,19},{19,3},{4,20},{20... | collective-permute-start | bytes 1671176 | tf_op jit(solution)/shard_map/ppermute | solution.py:539
  44.8 9.2 %collective-permute-start.13 = (f32[2,2,128,128]{3,2,1,0:T(8,128)S(1)}, f32[2,2,128,128]{3,2,1,0:T(8,128)S(1)}, u32[]{:S(2)}, u32[]{:S(2)}) collective-permute-start(f32[2,2,128,128]{3,2,1,0:T(8,128)S(1)} %get-tuple-element.48), channel_id=1, source_target_pairs={{0,2},{2,0},{4,6},{6,4},{8,10},{10,8},{12,14},{14,12},{1,3},{3,1},... | collective-permute-start | bytes 786440 | tf_op jit(solution)/shard_map/ppermute | solution.py:534
  44.8 17.7 %collective-permute-start.17 = (f32[2,6,64,128]{3,2,1,0:T(8,128)S(1)}, f32[2,6,64,128]{3,2,1,0:T(8,128)S(1)}, u32[]{:S(2)}, u32[]{:S(2)}) collective-permute-start(f32[2,6,64,128]{3,2,1,0:T(8,128)S(1)} %get-tuple-element.55), channel_id=1, source_target_pairs={{0,2},{2,0},{4,6},{6,4},{8,10},{10,8},{12,14},{14,12},{1,3},{3,1},... | collective-permute-start | bytes 1179656 | tf_op jit(solution)/shard_map/ppermute | solution.py:535
  46.9 8.4 %collective-permute-start.11 = (f32[4,136,128]{2,1,0:T(8,128)S(1)}, f32[4,136,128]{2,1,0:T(8,128)S(1)}, u32[]{:S(2)}, u32[]{:S(2)}) collective-permute-start(f32[4,136,128]{2,1,0:T(8,128)S(1)} %get-tuple-element.45), channel_id=1, source_target_pairs={{4,0},{8,4},{12,8},{2,6},{6,10},{10,14},{5,1},{9,5},{13,9},{3,7},{... | collective-permute-start | bytes 835592 | tf_op jit(solution)/shard_map/ppermute | solution.py:511
  54.1 14.0 %collective-permute-start.15 = (f32[2,6,64,128]{3,2,1,0:T(8,128)S(1)}, f32[2,6,64,128]{3,2,1,0:T(8,128)S(1)}, u32[]{:S(2)}, u32[]{:S(2)}) collective-permute-start(f32[2,6,64,128]{3,2,1,0:T(8,128)S(1)} %get-tuple-element.52), channel_id=1, source_target_pairs={{0,2},{2,0},{4,6},{6,4},{8,10},{10,8},{12,14},{14,12},{1,3},{3,1},... | collective-permute-start | bytes 1179656 | tf_op jit(solution)/shard_map/ppermute | solution.py:540
  55.3 12.8 %collective-permute-start.12 = (f32[2,2,128,128]{3,2,1,0:T(8,128)S(1)}, f32[2,2,128,128]{3,2,1,0:T(8,128)S(1)}, u32[]{:S(2)}, u32[]{:S(2)}) collective-permute-start(f32[2,2,128,128]{3,2,1,0:T(8,128)S(1)} %get-tuple-element.47), channel_id=1, source_target_pairs={{0,4},{4,8},{8,12},{6,2},{10,6},{14,10},{1,5},{5,9},{9,13},{7,3},{... | collective-permute-start | bytes 786440 | tf_op jit(solution)/shard_map/ppermute | solution.py:537
  62.5 9.9 %collective-permute-start.18 = (f32[2,6,64,128]{3,2,1,0:T(8,128)S(1)}, f32[2,6,64,128]{3,2,1,0:T(8,128)S(1)}, u32[]{:S(2)}, u32[]{:S(2)}) collective-permute-start(f32[2,6,64,128]{3,2,1,0:T(8,128)S(1)} %collective-permute-done.17.args_5_.args_19_.args_21_), channel_id=1, source_target_pairs={{0,4},{4,8},{8,12},{6,2},{10,6},{14,10},{1,5},{5,9},{9,13},{7,3},{... | collective-permute-start | bytes 1179656 | tf_op jit(solution)/shard_map/ppermute | solution.py:541
  66.0 6.4 %collective-permute-start.14 = (f32[2,2,128,128]{3,2,1,0:T(8,128)S(1)}, f32[2,2,128,128]{3,2,1,0:T(8,128)S(1)}, u32[]{:S(2)}, u32[]{:S(2)}) collective-permute-start(f32[2,2,128,128]{3,2,1,0:T(8,128)S(1)} %collective-permute-done.8.args_2_.args_15_), channel_id=1, source_target_pairs={{0,2},{2,0},{4,6},{6,4},{8,10},{10,8},{12,14},{14,12},{1,3},{3,1},... | collective-permute-start | bytes 786440 | tf_op jit(solution)/shard_map/ppermute | solution.py:538
  66.1 8.0 %copy-start.2 = (f32[2,6,128,128]{3,2,1,0:T(8,128)}, f32[2,6,128,128]{3,2,1,0:T(8,128)S(1)}, u32[]{:S(2)}) copy-start(f32[2,6,128,128]{3,2,1,0:T(8,128)S(1)} %collective-permute-done.9.args_5_) | copy-start | bytes 2359300
  67.5 6.5 %collective-permute-start.19 = (f32[106,8,128]{2,1,0:T(8,128)S(1)}, f32[106,8,128]{2,1,0:T(8,128)S(1)}, u32[]{:S(2)}, u32[]{:S(2)}) collective-permute-start(f32[106,8,128]{2,1,0:T(8,128)S(1)} %get-tuple-element.56), channel_id=1, source_target_pairs={{0,1},{1,0},{2,3},{3,2},{4,5},{5,4},{6,7},{7,6},{8,9},{9,8},{10,11... | collective-permute-start | bytes 1302536 | tf_op jit(solution)/shard_map/ppermute | solution.py:567
  68.1 12.7 %collective-permute-start.16 = (f32[2,6,64,128]{3,2,1,0:T(8,128)S(1)}, f32[2,6,64,128]{3,2,1,0:T(8,128)S(1)}, u32[]{:S(2)}, u32[]{:S(2)}) collective-permute-start(f32[2,6,64,128]{3,2,1,0:T(8,128)S(1)} %collective-permute-done.15.args_19_), channel_id=1, source_target_pairs={{0,4},{4,8},{8,12},{6,2},{10,6},{14,10},{1,5},{5,9},{9,13},{7,3},{... | collective-permute-start | bytes 1179656 | tf_op jit(solution)/shard_map/ppermute | solution.py:542
  72.5 1.6 %collective-permute-start.20 = (f32[2,28,8,128]{3,2,1,0:T(8,128)S(1)}, f32[2,28,8,128]{3,2,1,0:T(8,128)S(1)}, u32[]{:S(2)}, u32[]{:S(2)}) collective-permute-start(f32[2,28,8,128]{3,2,1,0:T(8,128)S(1)} %rim1.1), channel_id=1, source_target_pairs={{0,1},{1,0},{2,3},{3,2},{4,5},{5,4},{6,7},{7,6},{8,9},{9,8},{10,11... | collective-permute-start | bytes 688136 | tf_op jit(solution)/shard_map/ppermute | solution.py:577

commit v3 on v2

--- a/solution.py
+++ b/solution.py
@@ -8,7 +8,7 @@
 
 STEPS = 4
 LAG_HALF = 8
-CHUNKS = (64, 64)
+CHUNKS = (72, 56)
 
 
 def padded(cells, sides, width):
@@ -74,7 +74,7 @@
     return jnp.stack(image_lags)
 
 
-PARTS = 5
+PARTS = 7
 X = 8
 Y = 128
 Z = 128

time: 89.2 us -> 95 us (1.065)
  starting transfers between devices: 37.6 us -> 40 us
  Pallas kernels: 21.7 us -> 23.9 us
  waiting for transfers between devices: 29.2 us -> 30.2 us
    ppermute x1, waiting for transfers between devices: 5.92 us -> 11.1 us  [shards(): near_brow = lax.ppermute(after(brow, beside, near_mine), 'gx', swap_x)]
    ppermute x1, waiting for transfers between devices: 3.76 us -> 0.01 us  [shards(): near0 = lax.ppermute(after(parts[0], near_rest), 'gx', swap_x)]
    ppermute x1, waiting for transfers between devices: 0.01 us -> 2.85 us  [shards(): from_on1 = lax.ppermute(after(on1, near_rest), 'gx', onward)]
    pallas_call x7, Pallas kernels: 21.7 us -> 23.9 us  [call(): pl.pallas_call(kernel, out_shape=[jax.ShapeDtypeStruct(s, F32) for s in o...]
    ppermute x1, starting transfers between devices: 2.02 us -> 0.07 us  [shards(): near0 = lax.ppermute(after(parts[0], near_rest), 'gx', swap_x)]
    ppermute x1, starting transfers between devices: 0.01 us -> 1.95 us  [shards(): near_brow = lax.ppermute(after(brow, beside, near_mine), 'gx', swap_x)]
    ppermute x1, waiting for transfers between devices: 6.97 us -> 5.38 us  [shards(): from_back1 = lax.ppermute(brow, 'gx', backward)]
    ppermute x1, waiting for transfers between devices: 1.22 us -> 0.01 us  [shards(): from_back0 = lax.ppermute(after(back0, near_rest), 'gx', backward)]
  transfers between devices with their start and end apart: 21 -> 21, of which waited for: 9 -> 8; matrix products, arithmetic and copies ran while one was open for 0% -> 0% of each run, Pallas kernels for 14% -> 15%
where the time goes in v3:
time: 95 us; the launch traced here: 94.5 us
  starting transfers between devices  40 us (42%)
  waiting for transfers between devices  30.2 us (32%)
  Pallas kernels  23.9 us (25%)
    pallas_call x7, Pallas kernels, call(): pl.pallas_call(kernel, out_shape=[jax.ShapeDtypeStruct(s, F32) for s in o...  23.9 us
    ppermute x1, waiting for transfers between devices, shards(): near_brow = lax.ppermute(after(brow, beside, near_mine), 'gx', swap_x)  11.1 us
    ppermute x1, waiting for transfers between devices, shards(): near_edge = lax.ppermute(edge, 'gx', swap_x)  5.4 us
    ppermute x1, waiting for transfers between devices, shards(): from_back1 = lax.ppermute(brow, 'gx', backward)  5.38 us
    ppermute x1, starting transfers between devices, shards(): far1 = lax.ppermute(after(near1, from_on1, far_other), 'gx', onward)  4.58 us
    ppermute x1, starting transfers between devices, shards(): lax.ppermute(after(near_rest, far_mine, from_back1), 'gx', onward)  4.13 us
    ppermute x1, starting transfers between devices, shards(): far_edge = lax.ppermute(after(near_edge, beside), 'gx', onward)  4.05 us
    ppermute x1, starting transfers between devices, shards(): far_mine = lax.ppermute(after(near_mine, u1, from_on0), 'gx', onward)  3.52 us
  transfers between devices with their start and end apart: 21, of which 8 were waited for; matrix products, arithmetic and copies ran while one was open for 0% of the time, Pallas kernels for 15%

profile of v3, /device:TPU:0, one launch (start us, length us, event | category | flops | bytes accessed | tf_op | source)
XLA Modules:
  0.0 94.5 jit_solution(826020962481239630)
XLA Ops:
  0.0 1.0 %edge.1 = (f32[2,2,128,128]{3,2,1,0:T(8,128)S(1)}, f32[2,8,8,128]{3,2,1,0:T(8,128)S(1)}) custom-call(f32[2,8,128,128]{3,2,1,0:T(8,128)} %args_8_.7), custom_call_target="tpu_custom_call" | custom-call | tf_op jit(solution)/shard_map/edge/pallas_call | solution.py:462
  1.0 3.0 %collective-permute-start = (f32[2,2,128,128]{3,2,1,0:T(8,128)S(1)}, f32[2,2,128,128]{3,2,1,0:T(8,128)S(1)}, u32[]{:S(2)}, u32[]{:S(2)}) collective-permute-start(f32[2,2,128,128]{3,2,1,0:T(8,128)S(1)} %get-tuple-element.31), channel_id=1, source_target_pairs={{0,2},{2,0},{4,6},{6,4},{8,10},{10,8},{12,14},{14,12},{1,3},{3,1},... | collective-permute-start | bytes 786440 | tf_op jit(solution)/shard_map/ppermute | solution.py:505
  4.0 0.0 collective-permute-start.1
  4.0 1.5 %prep.1 = (f32[8,136,128]{2,1,0:T(8,128)S(1)}, f32[2,6,128,128]{3,2,1,0:T(8,128)S(1)}, f32[4,136,128]{2,1,0:T(8,128)S(1)}, f32[4,136,128]{2,1,0:T(8,128)S(1)}) custom-call(f32[2,8,128,128]{3,2,1,0:T(8,128)} %args_8_.7, f32[8,128,128]{2,1,0:T(8,128)} %args_9_.5, f32[8,128,128]{2,1,0:T(8,128)} %args_10_.5, f32[3,8,128]{2,1,0:T(8,128)} %args_13_.1, ...), custom_call_target="tpu_custom_call" | custom-call | tf_op jit(solution)/shard_map/prep/pallas_call | solution.py:462
  5.6 0.2 collective-permute-start.4
  5.7 0.0 collective-permute-done.1.args_6_
  5.7 5.4 %collective-permute-done.args_4_.args_0_ = f32[2,2,128,128]{3,2,1,0:T(8,128)S(1)} collective-permute-done((f32[2,2,128,128]{3,2,1,0:T(8,128)S(1)}, f32[2,2,128,128]{3,2,1,0:T(8,128)S(1)}, u32[]{:S(2)}, u32[]{:S(2)}) %collective-permute-start) | collective-permute-done | bytes 262176 | tf_op jit(solution)/shard_map/ppermute | solution.py:505
  11.1 4.1 %collective-permute-start.2 = (f32[2,2,128,128]{3,2,1,0:T(8,128)S(1)}, f32[2,2,128,128]{3,2,1,0:T(8,128)S(1)}, u32[]{:S(2)}, u32[]{:S(2)}) collective-permute-start(f32[2,2,128,128]{3,2,1,0:T(8,128)S(1)} %collective-permute-done.args_4_.args_0_), channel_id=1, source_target_pairs={{0,4},{4,8},{8,12},{6,2},{10,6},{14,10},{1,5},{5,9},{9,13},{7,3},{... | collective-permute-start | bytes 786440 | tf_op jit(solution)/shard_map/ppermute | solution.py:509
  15.2 3.5 %collective-permute-start.5 = (f32[4,136,128]{2,1,0:T(8,128)S(1)}, f32[4,136,128]{2,1,0:T(8,128)S(1)}, u32[]{:S(2)}, u32[]{:S(2)}) collective-permute-start(f32[4,136,128]{2,1,0:T(8,128)S(1)} %get-tuple-element.40), channel_id=1, source_target_pairs={{0,4},{4,8},{8,12},{6,2},{10,6},{14,10},{1,5},{5,9},{9,13},{7,3},{... | collective-permute-start | bytes 835592 | tf_op jit(solution)/shard_map/ppermute | solution.py:506
  18.7 3.1 %collective-permute-done.2.args_5_.args_4_ = f32[2,2,128,128]{3,2,1,0:T(8,128)S(1)} collective-permute-done((f32[2,2,128,128]{3,2,1,0:T(8,128)S(1)}, f32[2,2,128,128]{3,2,1,0:T(8,128)S(1)}, u32[]{:S(2)}, u32[]{:S(2)}) %collective-permute-start.2) | collective-permute-done | bytes 262176 | tf_op jit(solution)/shard_map/ppermute | solution.py:509
  21.8 2.3 %collective-permute-start.3 = (f32[2,6,128,128]{3,2,1,0:T(8,128)S(1)}, f32[2,6,128,128]{3,2,1,0:T(8,128)S(1)}, u32[]{:S(2)}, u32[]{:S(2)}) collective-permute-start(f32[2,6,128,128]{3,2,1,0:T(8,128)S(1)} %get-tuple-element.36), channel_id=1, source_target_pairs={{0,2},{2,0},{4,6},{6,4},{8,10},{10,8},{12,14},{14,12},{1,3},{3,1},... | collective-permute-start | bytes 2359304 | tf_op jit(solution)/shard_map/ppermute | solution.py:510
  24.1 3.0 %first.1 = (f32[2,8,128,128]{3,2,1,0:T(8,128)S(1)}, f32[2,2,128,128]{3,2,1,0:T(8,128)S(1)}, f32[2,2,128,128]{3,2,1,0:T(8,128)S(1)}, f32[2,6,72,128]{3,2,1,0:T(8,128)S(1)}, f32[2,6,56,128]{3,2,1,0:T(8,128)S(1)}) custom-call(f32[2,8,128,128]{3,2,1,0:T(8,128)} %args_8_.7, f32[2,8,128,128]{3,2,1,0:T(8,128)} %args_1_.4, f32[8,128,128]{2,1,0:T(8,128)} %args_9_.5, ...), custom_call_target="tpu_custom_call" | custom-call | tf_op jit(solution)/shard_map/first/pallas_call | solution.py:462
  27.1 0.0 collective-permute-done.5.args_11_
  27.1 0.0 collective-permute-done.4.args_2_
  27.2 3.5 %collective-permute-start.7 = (f32[8,136,128]{2,1,0:T(8,128)S(1)}, f32[8,136,128]{2,1,0:T(8,128)S(1)}, u32[]{:S(2)}, u32[]{:S(2)}) collective-permute-start(f32[8,136,128]{2,1,0:T(8,128)S(1)} %collective-permute-done.4.args_2_), channel_id=1, source_target_pairs={{0,4},{4,8},{8,12},{6,2},{10,6},{14,10},{1,5},{5,9},{9,13},{7,3},{... | collective-permute-start | bytes 1671176 | tf_op jit(solution)/shard_map/ppermute | solution.py:531
  30.7 1.3 %collective-permute-start.8 = (f32[2,2,128,128]{3,2,1,0:T(8,128)S(1)}, f32[2,2,128,128]{3,2,1,0:T(8,128)S(1)}, u32[]{:S(2)}, u32[]{:S(2)}) collective-permute-start(f32[2,2,128,128]{3,2,1,0:T(8,128)S(1)} %get-tuple-element.48), channel_id=1, source_target_pairs={{4,0},{8,4},{12,8},{2,6},{6,10},{10,14},{5,1},{9,5},{13,9},{3,7},{... | collective-permute-start | bytes 786440 | tf_op jit(solution)/shard_map/ppermute | solution.py:533
  32.0 1.6 %collective-permute-start.6 = (f32[8,136,128]{2,1,0:T(8,128)S(1)}, f32[8,136,128]{2,1,0:T(8,128)S(1)}, u32[]{:S(2)}, u32[]{:S(2)}) collective-permute-start(f32[8,136,128]{2,1,0:T(8,128)S(1)} %collective-permute-done.4.args_2_), channel_id=1, source_target_pairs={{0,16},{16,0},{1,17},{17,1},{2,18},{18,2},{3,19},{19,3},{4,20},{20... | collective-permute-start | bytes 1671176 | tf_op jit(solution)/shard_map/ppermute | solution.py:532
  33.6 5.4 %collective-permute-done.8.args_2_.args_15_ = f32[2,2,128,128]{3,2,1,0:T(8,128)S(1)} collective-permute-done((f32[2,2,128,128]{3,2,1,0:T(8,128)S(1)}, f32[2,2,128,128]{3,2,1,0:T(8,128)S(1)}, u32[]{:S(2)}, u32[]{:S(2)}) %collective-permute-start.8) | collective-permute-done | bytes 262176 | tf_op jit(solution)/shard_map/ppermute | solution.py:533
  39.0 0.0 collective-permute-done.7.args_6_
  39.0 0.1 collective-permute-done.3.args_1_
  39.1 4.1 %collective-permute-start.9 = (f32[2,6,128,128]{3,2,1,0:T(8,128)S(1)}, f32[2,6,128,128]{3,2,1,0:T(8,128)S(1)}, u32[]{:S(2)}, u32[]{:S(2)}) collective-permute-start(f32[2,6,128,128]{3,2,1,0:T(8,128)S(1)} %collective-permute-done.3.args_1_), channel_id=1, source_target_pairs={{0,4},{4,8},{8,12},{6,2},{10,6},{14,10},{1,5},{5,9},{9,13},{7,3},{... | collective-permute-start | bytes 2359304 | tf_op jit(solution)/shard_map/ppermute | solution.py:536
  43.2 0.1 collective-permute-start.17
  43.3 1.6 %collective-permute-start.10 = (f32[8,136,128]{2,1,0:T(8,128)S(1)}, f32[8,136,128]{2,1,0:T(8,128)S(1)}, u32[]{:S(2)}, u32[]{:S(2)}) collective-permute-start(f32[8,136,128]{2,1,0:T(8,128)S(1)} %collective-permute-done.7.args_6_), channel_id=1, source_target_pairs={{0,16},{16,0},{1,17},{17,1},{2,18},{18,2},{3,19},{19,3},{4,20},{20... | collective-permute-start | bytes 1671176 | tf_op jit(solution)/shard_map/ppermute | solution.py:539
  44.9 1.9 %collective-permute-start.13 = (f32[2,2,128,128]{3,2,1,0:T(8,128)S(1)}, f32[2,2,128,128]{3,2,1,0:T(8,128)S(1)}, u32[]{:S(2)}, u32[]{:S(2)}) collective-permute-start(f32[2,2,128,128]{3,2,1,0:T(8,128)S(1)} %get-tuple-element.48), channel_id=1, source_target_pairs={{0,2},{2,0},{4,6},{6,4},{8,10},{10,8},{12,14},{14,12},{1,3},{3,1},... | collective-permute-start | bytes 786440 | tf_op jit(solution)/shard_map/ppermute | solution.py:534
  46.9 0.0 collective-permute-done.6.args_3_
  46.9 1.3 %collective-permute-start.11 = (f32[4,136,128]{2,1,0:T(8,128)S(1)}, f32[4,136,128]{2,1,0:T(8,128)S(1)}, u32[]{:S(2)}, u32[]{:S(2)}) collective-permute-start(f32[4,136,128]{2,1,0:T(8,128)S(1)} %get-tuple-element.45), channel_id=1, source_target_pairs={{4,0},{8,4},{12,8},{2,6},{6,10},{10,14},{5,1},{9,5},{13,9},{3,7},{... | collective-permute-start | bytes 835592 | tf_op jit(solution)/shard_map/ppermute | solution.py:511
  48.1 11.1 %collective-permute-done.13.args_3_.args_16_ = f32[2,2,128,128]{3,2,1,0:T(8,128)S(1)} collective-permute-done((f32[2,2,128,128]{3,2,1,0:T(8,128)S(1)}, f32[2,2,128,128]{3,2,1,0:T(8,128)S(1)}, u32[]{:S(2)}, u32[]{:S(2)}) %collective-permute-start.13) | collective-permute-done | bytes 262176 | tf_op jit(solution)/shard_map/ppermute | solution.py:534
  59.3 0.0 collective-permute-start.15
  59.3 0.0 collective-permute-done.17.args_5_.args_19_.args_21_
  59.3 3.5 %collective-permute-start.18 = (f32[2,6,72,128]{3,2,1,0:T(8,128)S(1)}, f32[2,6,72,128]{3,2,1,0:T(8,128)S(1)}, u32[]{:S(2)}, u32[]{:S(2)}) collective-permute-start(f32[2,6,72,128]{3,2,1,0:T(8,128)S(1)} %collective-permute-done.17.args_5_.args_19_.args_21_), channel_id=1, source_target_pairs={{0,4},{4,8},{8,12},{6,2},{10,6},{14,10},{1,5},{5,9},{9,13},{7,3},{... | collective-permute-start | bytes 1327112 | tf_op jit(solution)/shard_map/ppermute | solution.py:541
  62.7 0.0 collective-permute-done.11.args_12_
  62.7 3.4 %collective-permute-start.12 = (f32[2,2,128,128]{3,2,1,0:T(8,128)S(1)}, f32[2,2,128,128]{3,2,1,0:T(8,128)S(1)}, u32[]{:S(2)}, u32[]{:S(2)}) collective-permute-start(f32[2,2,128,128]{3,2,1,0:T(8,128)S(1)} %get-tuple-element.47), channel_id=1, source_target_pairs={{0,4},{4,8},{8,12},{6,2},{10,6},{14,10},{1,5},{5,9},{9,13},{7,3},{... | collective-permute-start | bytes 786440 | tf_op jit(solution)/shard_map/ppermute | solution.py:537
  66.1 0.0 collective-permute-done.10.args_7_
  66.2 0.1 collective-permute-start.14
  66.2 0.0 collective-permute-done.9.args_5_
  66.3 1.5 %rim0.1 = (f32[106,8,128]{2,1,0:T(8,128)S(1)}, f32[2,128,128]{2,1,0:T(8,128)S(1)}) custom-call(f32[2,2,128,128]{3,2,1,0:T(8,128)S(1)} %collective-permute-done.args_4_.args_0_, f32[2,6,128,128]{3,2,1,0:T(8,128)S(1)} %collective-permute-done.3.args_1_, f32[8,136,128]{2,1,0:T(8,128)S(1)} %collective-permute-done.4.args_2_, ...), custom_call_target="tpu_custom_call" | custom-call | tf_op jit(solution)/shard_map/rim0/pallas_call | solution.py:462
  67.7 0.1 collective-permute-start.19
  67.8 0.7 collective-permute-done.15.args_19_
  68.5 2.8 %collective-permute-done.12.args_1_.args_14_ = f32[2,2,128,128]{3,2,1,0:T(8,128)S(1)} collective-permute-done((f32[2,2,128,128]{3,2,1,0:T(8,128)S(1)}, f32[2,2,128,128]{3,2,1,0:T(8,128)S(1)}, u32[]{:S(2)}, u32[]{:S(2)}) %collective-permute-start.12) | collective-permute-done | bytes 262176 | tf_op jit(solution)/shard_map/ppermute | solution.py:537
  71.3 4.6 %collective-permute-start.16 = (f32[2,6,56,128]{3,2,1,0:T(8,128)S(1)}, f32[2,6,56,128]{3,2,1,0:T(8,128)S(1)}, u32[]{:S(2)}, u32[]{:S(2)}) collective-permute-start(f32[2,6,56,128]{3,2,1,0:T(8,128)S(1)} %collective-permute-done.15.args_19_), channel_id=1, source_target_pairs={{0,4},{4,8},{8,12},{6,2},{10,6},{14,10},{1,5},{5,9},{9,13},{7,3},{... | collective-permute-start | bytes 1032200 | tf_op jit(solution)/shard_map/ppermute | solution.py:542
  75.9 0.0 collective-permute-done.14.args_4_.args_17_
  75.9 0.0 collective-permute-done.18.args_6_.args_20_.args_22_
  75.9 0.1 rim1.1
  76.1 0.1 collective-permute-start.20
  76.1 1.5 %collective-permute-done.20.args_22_ = f32[2,28,8,128]{3,2,1,0:T(8,128)S(1)} collective-permute-done((f32[2,28,8,128]{3,2,1,0:T(8,128)S(1)}, f32[2,28,8,128]{3,2,1,0:T(8,128)S(1)}, u32[]{:S(2)}, u32[]{:S(2)}) %collective-permute-start.20) | collective-permute-done | bytes 229408 | tf_op jit(solution)/shard_map/ppermute | solution.py:577
  77.6 0.0 collective-permute-done.19.args_21_
  77.6 8.4 %slab0.1.args_23_ = f32[17,8,128,128]{3,2,1,0:T(8,128)} custom-call(f32[2,2,128,128]{3,2,1,0:T(8,128)S(1)} %collective-permute-done.args_4_.args_0_, f32[2,6,128,128]{3,2,1,0:T(8,128)} %copy-done.1, f32[8,136,128]{2,1,0:T(8,128)S(1)} %collective-permute-done.4.args_2_, f32[8,136,128]{2,1,0:T(8,128)S(1)} %collective-permute-done.6.args_3_, ...), custom_call_target="tpu_custom_call" | custom-call | tf_op jit(solution)/shard_map/slab0/pallas_call | solution.py:462
  86.0 8.3 %slab1.1 = f32[17,8,128,128]{3,2,1,0:T(8,128)} custom-call(f32[2,2,128,128]{3,2,1,0:T(8,128)S(1)} %collective-permute-done.args_4_.args_0_, f32[2,6,128,128]{3,2,1,0:T(8,128)} %copy-done.1, f32[8,136,128]{2,1,0:T(8,128)S(1)} %collective-permute-done.4.args_2_, f32[8,136,128]{2,1,0:T(8,128)S(1)} %collective-permute-done.6.args_3_, ...), custom_call_target="tpu_custom_call", output_to_operand_aliasing={{}: (23, {})} | custom-call | tf_op jit(solution)/shard_map/slab1/pallas_call | solution.py:462
  (7 shorter events, 0.0 us)
Async XLA Ops:
  1.0 10.1 %collective-permute-start = (f32[2,2,128,128]{3,2,1,0:T(8,128)S(1)}, f32[2,2,128,128]{3,2,1,0:T(8,128)S(1)}, u32[]{:S(2)}, u32[]{:S(2)}) collective-permute-start(f32[2,2,128,128]{3,2,1,0:T(8,128)S(1)} %get-tuple-element.31), channel_id=1, source_target_pairs={{0,2},{2,0},{4,6},{6,4},{8,10},{10,8},{12,14},{14,12},{1,3},{3,1},... | collective-permute-start | bytes 786440 | tf_op jit(solution)/shard_map/ppermute | solution.py:505
  4.0 1.7 %collective-permute-start.1 = (f32[2,8,8,128]{3,2,1,0:T(8,128)S(1)}, f32[2,8,8,128]{3,2,1,0:T(8,128)S(1)}, u32[]{:S(2)}, u32[]{:S(2)}) collective-permute-start(f32[2,8,8,128]{3,2,1,0:T(8,128)S(1)} %get-tuple-element.32), channel_id=1, source_target_pairs={{0,1},{1,0},{2,3},{3,2},{4,5},{5,4},{6,7},{7,6},{8,9},{9,8},{10,11... | collective-permute-start | bytes 196616 | tf_op jit(solution)/shard_map/ppermute | solution.py:507
  5.6 21.6 %collective-permute-start.4 = (f32[8,136,128]{2,1,0:T(8,128)S(1)}, f32[8,136,128]{2,1,0:T(8,128)S(1)}, u32[]{:S(2)}, u32[]{:S(2)}) collective-permute-start(f32[8,136,128]{2,1,0:T(8,128)S(1)} %get-tuple-element.37), channel_id=1, source_target_pairs={{0,2},{2,0},{4,6},{6,4},{8,10},{10,8},{12,14},{14,12},{1,3},{3,1},... | collective-permute-start | bytes 1671176 | tf_op jit(solution)/shard_map/ppermute | solution.py:508
  11.1 10.7 %collective-permute-start.2 = (f32[2,2,128,128]{3,2,1,0:T(8,128)S(1)}, f32[2,2,128,128]{3,2,1,0:T(8,128)S(1)}, u32[]{:S(2)}, u32[]{:S(2)}) collective-permute-start(f32[2,2,128,128]{3,2,1,0:T(8,128)S(1)} %collective-permute-done.args_4_.args_0_), channel_id=1, source_target_pairs={{0,4},{4,8},{8,12},{6,2},{10,6},{14,10},{1,5},{5,9},{9,13},{7,3},{... | collective-permute-start | bytes 786440 | tf_op jit(solution)/shard_map/ppermute | solution.py:509
  15.2 11.9 %collective-permute-start.5 = (f32[4,136,128]{2,1,0:T(8,128)S(1)}, f32[4,136,128]{2,1,0:T(8,128)S(1)}, u32[]{:S(2)}, u32[]{:S(2)}) collective-permute-start(f32[4,136,128]{2,1,0:T(8,128)S(1)} %get-tuple-element.40), channel_id=1, source_target_pairs={{0,4},{4,8},{8,12},{6,2},{10,6},{14,10},{1,5},{5,9},{9,13},{7,3},{... | collective-permute-start | bytes 835592 | tf_op jit(solution)/shard_map/ppermute | solution.py:506
  21.8 17.3 %collective-permute-start.3 = (f32[2,6,128,128]{3,2,1,0:T(8,128)S(1)}, f32[2,6,128,128]{3,2,1,0:T(8,128)S(1)}, u32[]{:S(2)}, u32[]{:S(2)}) collective-permute-start(f32[2,6,128,128]{3,2,1,0:T(8,128)S(1)} %get-tuple-element.36), channel_id=1, source_target_pairs={{0,2},{2,0},{4,6},{6,4},{8,10},{10,8},{12,14},{14,12},{1,3},{3,1},... | collective-permute-start | bytes 2359304 | tf_op jit(solution)/shard_map/ppermute | solution.py:510
  27.1 50.5 %copy-start = (f32[2,8,128,128]{3,2,1,0:T(8,128)}, f32[2,8,128,128]{3,2,1,0:T(8,128)S(1)}, u32[]{:S(2)}) copy-start(f32[2,8,128,128]{3,2,1,0:T(8,128)S(1)} %get-tuple-element.38.args_0_.args_13_) | copy-start | bytes 3145732
  27.2 11.8 %collective-permute-start.7 = (f32[8,136,128]{2,1,0:T(8,128)S(1)}, f32[8,136,128]{2,1,0:T(8,128)S(1)}, u32[]{:S(2)}, u32[]{:S(2)}) collective-permute-start(f32[8,136,128]{2,1,0:T(8,128)S(1)} %collective-permute-done.4.args_2_), channel_id=1, source_target_pairs={{0,4},{4,8},{8,12},{6,2},{10,6},{14,10},{1,5},{5,9},{9,13},{7,3},{... | collective-permute-start | bytes 1671176 | tf_op jit(solution)/shard_map/ppermute | solution.py:531
  30.7 8.3 %collective-permute-start.8 = (f32[2,2,128,128]{3,2,1,0:T(8,128)S(1)}, f32[2,2,128,128]{3,2,1,0:T(8,128)S(1)}, u32[]{:S(2)}, u32[]{:S(2)}) collective-permute-start(f32[2,2,128,128]{3,2,1,0:T(8,128)S(1)} %get-tuple-element.48), channel_id=1, source_target_pairs={{4,0},{8,4},{12,8},{2,6},{6,10},{10,14},{5,1},{9,5},{13,9},{3,7},{... | collective-permute-start | bytes 786440 | tf_op jit(solution)/shard_map/ppermute | solution.py:533
  32.0 14.9 %collective-permute-start.6 = (f32[8,136,128]{2,1,0:T(8,128)S(1)}, f32[8,136,128]{2,1,0:T(8,128)S(1)}, u32[]{:S(2)}, u32[]{:S(2)}) collective-permute-start(f32[8,136,128]{2,1,0:T(8,128)S(1)} %collective-permute-done.4.args_2_), channel_id=1, source_target_pairs={{0,16},{16,0},{1,17},{17,1},{2,18},{18,2},{3,19},{19,3},{4,20},{20... | collective-permute-start | bytes 1671176 | tf_op jit(solution)/shard_map/ppermute | solution.py:532
  39.1 38.5 %copy-start.1 = (f32[2,6,128,128]{3,2,1,0:T(8,128)}, f32[2,6,128,128]{3,2,1,0:T(8,128)S(1)}, u32[]{:S(2)}) copy-start(f32[2,6,128,128]{3,2,1,0:T(8,128)S(1)} %collective-permute-done.3.args_1_) | copy-start | bytes 2359300
  39.1 27.1 %collective-permute-start.9 = (f32[2,6,128,128]{3,2,1,0:T(8,128)S(1)}, f32[2,6,128,128]{3,2,1,0:T(8,128)S(1)}, u32[]{:S(2)}, u32[]{:S(2)}) collective-permute-start(f32[2,6,128,128]{3,2,1,0:T(8,128)S(1)} %collective-permute-done.3.args_1_), channel_id=1, source_target_pairs={{0,4},{4,8},{8,12},{6,2},{10,6},{14,10},{1,5},{5,9},{9,13},{7,3},{... | collective-permute-start | bytes 2359304 | tf_op jit(solution)/shard_map/ppermute | solution.py:536
  43.2 16.0 %collective-permute-start.17 = (f32[2,6,72,128]{3,2,1,0:T(8,128)S(1)}, f32[2,6,72,128]{3,2,1,0:T(8,128)S(1)}, u32[]{:S(2)}, u32[]{:S(2)}) collective-permute-start(f32[2,6,72,128]{3,2,1,0:T(8,128)S(1)} %get-tuple-element.55), channel_id=1, source_target_pairs={{0,2},{2,0},{4,6},{6,4},{8,10},{10,8},{12,14},{14,12},{1,3},{3,1},... | collective-permute-start | bytes 1327112 | tf_op jit(solution)/shard_map/ppermute | solution.py:535
  43.3 22.8 %collective-permute-start.10 = (f32[8,136,128]{2,1,0:T(8,128)S(1)}, f32[8,136,128]{2,1,0:T(8,128)S(1)}, u32[]{:S(2)}, u32[]{:S(2)}) collective-permute-start(f32[8,136,128]{2,1,0:T(8,128)S(1)} %collective-permute-done.7.args_6_), channel_id=1, source_target_pairs={{0,16},{16,0},{1,17},{17,1},{2,18},{18,2},{3,19},{19,3},{4,20},{20... | collective-permute-start | bytes 1671176 | tf_op jit(solution)/shard_map/ppermute | solution.py:539
  44.9 14.4 %collective-permute-start.13 = (f32[2,2,128,128]{3,2,1,0:T(8,128)S(1)}, f32[2,2,128,128]{3,2,1,0:T(8,128)S(1)}, u32[]{:S(2)}, u32[]{:S(2)}) collective-permute-start(f32[2,2,128,128]{3,2,1,0:T(8,128)S(1)} %get-tuple-element.48), channel_id=1, source_target_pairs={{0,2},{2,0},{4,6},{6,4},{8,10},{10,8},{12,14},{14,12},{1,3},{3,1},... | collective-permute-start | bytes 786440 | tf_op jit(solution)/shard_map/ppermute | solution.py:534
  46.9 15.9 %collective-permute-start.11 = (f32[4,136,128]{2,1,0:T(8,128)S(1)}, f32[4,136,128]{2,1,0:T(8,128)S(1)}, u32[]{:S(2)}, u32[]{:S(2)}) collective-permute-start(f32[4,136,128]{2,1,0:T(8,128)S(1)} %get-tuple-element.45), channel_id=1, source_target_pairs={{4,0},{8,4},{12,8},{2,6},{6,10},{10,14},{5,1},{9,5},{13,9},{3,7},{... | collective-permute-start | bytes 835592 | tf_op jit(solution)/shard_map/ppermute | solution.py:511
  59.3 9.2 %collective-permute-start.15 = (f32[2,6,56,128]{3,2,1,0:T(8,128)S(1)}, f32[2,6,56,128]{3,2,1,0:T(8,128)S(1)}, u32[]{:S(2)}, u32[]{:S(2)}) collective-permute-start(f32[2,6,56,128]{3,2,1,0:T(8,128)S(1)} %get-tuple-element.52), channel_id=1, source_target_pairs={{0,2},{2,0},{4,6},{6,4},{8,10},{10,8},{12,14},{14,12},{1,3},{3,1},... | collective-permute-start | bytes 1032200 | tf_op jit(solution)/shard_map/ppermute | solution.py:540
  59.3 16.6 %collective-permute-start.18 = (f32[2,6,72,128]{3,2,1,0:T(8,128)S(1)}, f32[2,6,72,128]{3,2,1,0:T(8,128)S(1)}, u32[]{:S(2)}, u32[]{:S(2)}) collective-permute-start(f32[2,6,72,128]{3,2,1,0:T(8,128)S(1)} %collective-permute-done.17.args_5_.args_19_.args_21_), channel_id=1, source_target_pairs={{0,4},{4,8},{8,12},{6,2},{10,6},{14,10},{1,5},{5,9},{9,13},{7,3},{... | collective-permute-start | bytes 1327112 | tf_op jit(solution)/shard_map/ppermute | solution.py:541
  62.7 8.6 %collective-permute-start.12 = (f32[2,2,128,128]{3,2,1,0:T(8,128)S(1)}, f32[2,2,128,128]{3,2,1,0:T(8,128)S(1)}, u32[]{:S(2)}, u32[]{:S(2)}) collective-permute-start(f32[2,2,128,128]{3,2,1,0:T(8,128)S(1)} %get-tuple-element.47), channel_id=1, source_target_pairs={{0,4},{4,8},{8,12},{6,2},{10,6},{14,10},{1,5},{5,9},{9,13},{7,3},{... | collective-permute-start | bytes 786440 | tf_op jit(solution)/shard_map/ppermute | solution.py:537
  66.2 9.7 %collective-permute-start.14 = (f32[2,2,128,128]{3,2,1,0:T(8,128)S(1)}, f32[2,2,128,128]{3,2,1,0:T(8,128)S(1)}, u32[]{:S(2)}, u32[]{:S(2)}) collective-permute-start(f32[2,2,128,128]{3,2,1,0:T(8,128)S(1)} %collective-permute-done.8.args_2_.args_15_), channel_id=1, source_target_pairs={{0,2},{2,0},{4,6},{6,4},{8,10},{10,8},{12,14},{14,12},{1,3},{3,1},... | collective-permute-start | bytes 786440 | tf_op jit(solution)/shard_map/ppermute | solution.py:538
  66.2 11.4 %copy-start.2 = (f32[2,6,128,128]{3,2,1,0:T(8,128)}, f32[2,6,128,128]{3,2,1,0:T(8,128)S(1)}, u32[]{:S(2)}) copy-start(f32[2,6,128,128]{3,2,1,0:T(8,128)S(1)} %collective-permute-done.9.args_5_) | copy-start | bytes 2359300
  67.7 9.9 %collective-permute-start.19 = (f32[106,8,128]{2,1,0:T(8,128)S(1)}, f32[106,8,128]{2,1,0:T(8,128)S(1)}, u32[]{:S(2)}, u32[]{:S(2)}) collective-permute-start(f32[106,8,128]{2,1,0:T(8,128)S(1)} %get-tuple-element.56), channel_id=1, source_target_pairs={{0,1},{1,0},{2,3},{3,2},{4,5},{5,4},{6,7},{7,6},{8,9},{9,8},{10,11... | collective-permute-start | bytes 1302536 | tf_op jit(solution)/shard_map/ppermute | solution.py:567
  71.3 14.7 %collective-permute-start.16 = (f32[2,6,56,128]{3,2,1,0:T(8,128)S(1)}, f32[2,6,56,128]{3,2,1,0:T(8,128)S(1)}, u32[]{:S(2)}, u32[]{:S(2)}) collective-permute-start(f32[2,6,56,128]{3,2,1,0:T(8,128)S(1)} %collective-permute-done.15.args_19_), channel_id=1, source_target_pairs={{0,4},{4,8},{8,12},{6,2},{10,6},{14,10},{1,5},{5,9},{9,13},{7,3},{... | collective-permute-start | bytes 1032200 | tf_op jit(solution)/shard_map/ppermute | solution.py:542
  76.1 1.6 %collective-permute-start.20 = (f32[2,28,8,128]{3,2,1,0:T(8,128)S(1)}, f32[2,28,8,128]{3,2,1,0:T(8,128)S(1)}, u32[]{:S(2)}, u32[]{:S(2)}) collective-permute-start(f32[2,28,8,128]{3,2,1,0:T(8,128)S(1)} %rim1.1), channel_id=1, source_target_pairs={{0,1},{1,0},{2,3},{3,2},{4,5},{5,4},{6,7},{7,6},{8,9},{9,8},{10,11... | collective-permute-start | bytes 688136 | tf_op jit(solution)/shard_map/ppermute | solution.py:577
